TPU v7x, 32 devices: a whole 2x2x4 slice. The times are simulated.
32 devices in a mesh: leaf: 8 (over y, x, core), panel: 4 (over z).
Axes of the slice: x: 2, y: 2, z: 4, core: 2. Of those that a mesh axis runs over, the one named last changes fastest.
Arguments:
- live_tiles: int32 [15], replicated, may hold values from 8 to 16
- row_tiles: int32 [14, 8], replicated, may hold values from 0 to 47, as said below
- rhs0: float32 [256, 16384], P('panel', 'leaf'), may hold values from -6 to 6
- rhs1: float32 [256, 8192], P('panel', 'leaf'), may hold values from -6 to 6
- rhs2: float32 [256, 4096], P('panel', 'leaf'), may hold values from -6 to 6
- rhs3: float32 [256, 2048], P('panel', 'leaf'), may hold values from -6 to 6
- dinv0: float32 [16384, 2048], P('leaf', 'panel'), as said below
- dinv1: float32 [8192, 2048], P('leaf', 'panel'), as said below
- dinv2: float32 [4096, 2048], P('leaf', 'panel'), as said below
- dinv3: float32 [2048, 2048], P('leaf', 'panel'), as said below
- off0: float32 [8192, 2048], P('leaf', 'panel'), may hold values from -0.125 to 0.125
- off1: float32 [4096, 2048], P('leaf', 'panel'), may hold values from -0.125 to 0.125
- off2: float32 [2048, 2048], P('leaf', 'panel'), may hold values from -0.125 to 0.125
Outputs:
- sol0: float32 [256, 16384], P('panel', 'leaf')
- sol1: float32 [256, 8192], P('panel', 'leaf')
- sol2: float32 [256, 4096], P('panel', 'leaf')
- sol3: float32 [256, 2048], P('panel', 'leaf')
Inputs may be any that keep to these rules, and one draw needn't show every extreme that they name: `row_tiles`: each row names 8 different tiles; for a supernode of level k every value is below (3 - k) * 16. `live_tiles`: counted level by level in the supernodes' order. `dinv0`: each 2048 x 2048 row block is lower triangular with diagonal entries from 0.5 to 2. `dinv1`: each 2048 x 2048 row block is lower triangular with diagonal entries from 0.5 to 2. `dinv2`: each 2048 x 2048 row block is lower triangular with diagonal entries from 0.5 to 2. `dinv3`: each 2048 x 2048 row block is lower triangular with diagonal entries from 0.5 to 2.
All inputs are finite; a program needn't handle non-finite values.
Results may differ from a plain program's by a relative error of at most 0.00028.
Values sent between devices are 32-bit elements; how exact they have to be, the bound alone decides.
A program may use at most 64 MiB of HBM per device.

v0:
```python
import jax
import jax.numpy as jnp
from jax import lax
from jax.sharding import PartitionSpec as P

B = 128
LEVELS = 4


highest = lax.Precision.HIGHEST


def swapped(block, axis, bit):
    count = lax.axis_size(axis)
    route = []
    for low in range(count):
        high = low | 1 << bit
        if high != low and high < count:
            route += [(low, high), (high, low)]
    return lax.ppermute(block, axis, route)


def leaf_bit(leaf_index, bit_number):
    return leaf_index // 2**bit_number % 2


def group_rows(vector, height, leaf_index):
    for bit_number in range(height):
        partner = swapped(vector, "leaf", bit_number)
        is_lower = leaf_bit(leaf_index, bit_number) == 0
        vector = jnp.where(
            is_lower, jnp.concatenate([vector, partner], 1), jnp.concatenate([partner, vector], 1)
        )
    return vector


def group_halving(buffer, height, leaf_index):
    for bit_number in reversed(range(height)):
        half_width = buffer.shape[1] // 2
        is_lower = leaf_bit(leaf_index, bit_number) == 0
        kept_half = jnp.where(is_lower, buffer[:, :half_width], buffer[:, half_width:])
        given_half = jnp.where(is_lower, buffer[:, half_width:], buffer[:, :half_width])
        buffer = kept_half + swapped(given_half, "leaf", bit_number)
    return buffer


def group_total(partial_sum, height):
    for bit_number in range(height):
        partial_sum = partial_sum + swapped(partial_sum, "leaf", bit_number)
    return partial_sum


def to_columns(vector, height, leaf_index):
    full_rows = group_rows(vector, height, leaf_index)
    return lax.all_to_all(full_rows, "panel", split_axis=1, concat_axis=0, tiled=True)


def contract_last(left, right):
    return lax.dot_general(
        left, right, (((1,), (1,)), ((), ())), precision=highest, preferred_element_type=jnp.float32
    )


def selector(chosen, offset, tile_count):
    return (chosen[:, None] == offset + jnp.arange(tile_count, dtype=jnp.int32)[None, :]).astype(
        jnp.float32
    )


def geometry(height, leaf_index, live_tiles, first_node, order_rows):
    group_width = 2**height
    node_index = leaf_index // group_width
    group_place = leaf_index % group_width
    rows_here = order_rows // group_width
    live_count = lax.dynamic_index_in_dim(live_tiles, first_node + node_index, keepdims=False)
    node_mask = (jnp.arange(order_rows, dtype=jnp.int32) < live_count * B).astype(jnp.float32)
    local_mask = lax.dynamic_slice_in_dim(node_mask, group_place * rows_here, rows_here)
    return (node_index, group_place, rows_here, node_mask, local_mask)


def chosen_tiles(row_tiles, first_node, node_index, group_place, local_tiles):
    entry = lax.dynamic_index_in_dim(row_tiles, first_node + node_index, keepdims=False)
    return lax.dynamic_slice_in_dim(entry, group_place * local_tiles, local_tiles)


def local(
    live_tiles, row_tiles, rhs0, rhs1, rhs2, rhs3, dinv0, dinv1, dinv2, dinv3, off0, off1, off2
):
    right_sides = [rhs0, rhs1, rhs2, rhs3]
    inverses = [dinv0, dinv1, dinv2, dinv3]
    off_rows = [off0, off1, off2]
    leaf_index = lax.axis_index("leaf")
    panel_index = lax.axis_index("panel")
    leaf_count = lax.axis_size("leaf")
    panel_count = lax.axis_size("panel")
    order_rows = dinv0.shape[0]
    tile_count = order_rows // B
    share_rows = rhs0.shape[0]
    all_rhs = share_rows * panel_count
    off_tiles = row_tiles.shape[1]
    first_nodes = []
    start_node = 0
    for height in range(LEVELS):
        first_nodes.append(start_node)
        start_node = start_node + leaf_count // 2**height
    buffers = [jnp.zeros((share_rows, order_rows), jnp.float32) for height in range(LEVELS)]
    columns_kept = []
    for height in range(LEVELS):
        node_index, group_place, rows_here, node_mask, local_mask = geometry(
            height, leaf_index, live_tiles, first_nodes[height], order_rows
        )
        residual = right_sides[height]
        if height > 0:
            residual = residual - group_halving(buffers[height], height, leaf_index)
        spread = to_columns(residual * local_mask[None, :], height, leaf_index)
        inverse = inverses[height]
        solved = lax.psum_scatter(
            contract_last(spread, inverse), "panel", scatter_dimension=0, tiled=True
        )
        columns = to_columns(solved * local_mask[None, :], height, leaf_index)
        columns_kept.append(columns)
        if height < LEVELS - 1:
            block_rows = off_rows[height]
            update = lax.psum_scatter(
                contract_last(columns, block_rows), "panel", scatter_dimension=0, tiled=True
            )
            local_tiles = off_tiles // 2**height
            chosen = chosen_tiles(
                row_tiles, first_nodes[height], node_index, group_place, local_tiles
            )
            pieces = update.reshape(share_rows, local_tiles, B)
            for ancestor in range(height + 1, LEVELS):
                picked = selector(chosen, (ancestor - height - 1) * tile_count, tile_count)
                sent = jnp.einsum("rtb,tc->rcb", pieces, picked, precision=highest)
                buffers[ancestor] = buffers[ancestor] + sent.reshape(share_rows, order_rows)
    full_solutions = [None] * LEVELS
    outputs = [None] * LEVELS
    for height in reversed(range(LEVELS)):
        node_index, group_place, rows_here, node_mask, local_mask = geometry(
            height, leaf_index, live_tiles, first_nodes[height], order_rows
        )
        target = columns_kept[height]
        if height < LEVELS - 1:
            local_tiles = off_tiles // 2**height
            chosen = chosen_tiles(
                row_tiles, first_nodes[height], node_index, group_place, local_tiles
            )
            gathered = jnp.zeros((all_rhs, local_tiles, B), jnp.float32)
            for ancestor in range(height + 1, LEVELS):
                picked = selector(chosen, (ancestor - height - 1) * tile_count, tile_count)
                above = full_solutions[ancestor].reshape(all_rhs, tile_count, B)
                gathered = gathered + jnp.einsum("rcb,tc->rtb", above, picked, precision=highest)
            correction = jnp.dot(
                gathered.reshape(all_rhs, local_tiles * B),
                off_rows[height],
                precision=highest,
                preferred_element_type=jnp.float32,
            )
            target = target - group_total(correction, height)
        whole_target = lax.all_gather(target, "panel", axis=1, tiled=True) * node_mask[None, :]
        mine = lax.dynamic_slice_in_dim(whole_target, group_place * rows_here, rows_here, 1)
        partial_sum = jnp.dot(
            mine, inverses[height], precision=highest, preferred_element_type=jnp.float32
        )
        partial_sum = group_total(partial_sum, height)
        whole_solution = (
            lax.all_gather(partial_sum, "panel", axis=1, tiled=True) * node_mask[None, :]
        )
        full_solutions[height] = whole_solution
        outputs[height] = lax.dynamic_slice(
            whole_solution,
            (panel_index * share_rows, group_place * rows_here),
            (share_rows, rows_here),
        )
    return tuple(outputs)


def solution(mesh):
    return jax.shard_map(
        local,
        mesh=mesh,
        in_specs=(
            P(),
            P(),
            P("panel", "leaf"),
            P("panel", "leaf"),
            P("panel", "leaf"),
            P("panel", "leaf"),
            P("leaf", "panel"),
            P("leaf", "panel"),
            P("leaf", "panel"),
            P("leaf", "panel"),
            P("leaf", "panel"),
            P("leaf", "panel"),
            P("leaf", "panel"),
        ),
        out_specs=(P("panel", "leaf"), P("panel", "leaf"), P("panel", "leaf"), P("panel", "leaf")),
        check_vma=False,
    )
```

profile of v0, /device:TPU:0, one launch (start us, length us, event | category | flops | bytes accessed | tf_op | source)
XLA Modules:
  0.0 910.1 jit_solution(4213799960495342376)
XLA Ops:
  10.6 20.6 %all_to_all.134 = f32[64,4,512]{2,0,1:T(8,128)S(1)} all-to-all(f32[64,4,512]{2,0,1:T(8,128)S(1)} %bitcast.207), channel_id=1, replica_groups=mesh['leaf'=8,'panel'=4] {'panel'}, dimensions={1} | all-to-all | bytes 1048576 | tf_op jit(solution)/shard_map/all_to_all | solution.py:55
  31.2 7.1 fusion.71
  38.4 42.8 %reduce-scatter.8.cloned.1.call-done = f32[64,2048]{1,0:T(8,128)} async-done(((f32[256,2048]{1,0:T(8,128)}), f32[64,2048]{1,0:T(8,128)}) %reduce-scatter.8.cloned.1.call-update) | async-done | bytes 524304 | tf_op jit(solution)/shard_map/reduce_scatter | solution.py:117
  82.6 17.5 %all_to_all.135 = f32[64,4,512]{2,0,1:T(8,128)S(1)} all-to-all(f32[64,4,512]{2,0,1:T(8,128)S(1)} %bitcast.209), channel_id=1, replica_groups=mesh['leaf'=8,'panel'=4] {'panel'}, dimensions={1} | all-to-all | bytes 1048576 | tf_op jit(solution)/shard_map/all_to_all | solution.py:55
  100.0 2.9 fusion.72
  103.2 25.9 %reduce-scatter.10.cloned.1.call-done = f32[64,1024]{1,0:T(8,128)} async-done(((f32[256,1024]{1,0:T(8,128)}), f32[64,1024]{1,0:T(8,128)}) %reduce-scatter.10.cloned.1.call-update) | async-done | bytes 262160 | tf_op jit(solution)/shard_map/reduce_scatter | solution.py:124
  136.2 17.5 %all_to_all.136 = f32[64,4,512]{2,0,1:T(8,128)S(1)} all-to-all(f32[64,4,512]{2,0,1:T(8,128)S(1)} %maximum_select_fusion), channel_id=1, replica_groups=mesh['leaf'=8,'panel'=4] {'panel'}, dimensions={1} | all-to-all | bytes 1048576 | tf_op jit(solution)/shard_map/all_to_all | solution.py:55
  153.6 2.9 fusion.73
  156.7 26.4 %reduce-scatter.12.cloned.1.call-done = f32[64,1024]{1,0:T(8,128)} async-done(((f32[256,1024]{1,0:T(8,128)}), f32[64,1024]{1,0:T(8,128)}) %reduce-scatter.12.cloned.1.call-update) | async-done | bytes 262160 | tf_op jit(solution)/shard_map/reduce_scatter | solution.py:117
  185.8 17.5 %all_to_all.137 = f32[64,4,512]{2,0,1:T(8,128)S(1)} all-to-all(f32[64,4,512]{2,0,1:T(8,128)S(1)} %maximum_select_fusion.1), channel_id=1, replica_groups=mesh['leaf'=8,'panel'=4] {'panel'}, dimensions={1} | all-to-all | bytes 1048576 | tf_op jit(solution)/shard_map/all_to_all | solution.py:55
  204.1 1.9 fusion.74
  207.5 19.5 %reduce-scatter.14.cloned.1.call-done = f32[64,512]{1,0:T(8,128)} async-done(((f32[256,512]{1,0:T(8,128)}), f32[64,512]{1,0:T(8,128)}) %reduce-scatter.14.cloned.1.call-update) | async-done | bytes 131088 | tf_op jit(solution)/shard_map/reduce_scatter | solution.py:124
  230.8 5.0 collective-permute-done.3
  239.7 1.6 collective-permute-start.6
  241.3 6.9 collective-permute-done.6
  248.3 16.7 %all_to_all.138 = f32[64,4,512]{2,0,1:T(8,128)S(1)} all-to-all(f32[64,4,512]{2,0,1:T(8,128)S(1)} %maximum_select_fusion.2), channel_id=1, replica_groups=mesh['leaf'=8,'panel'=4] {'panel'}, dimensions={1} | all-to-all | bytes 1048576 | tf_op jit(solution)/shard_map/all_to_all | solution.py:55
  265.0 1.9 fusion.75
  267.0 21.0 %reduce-scatter.16.cloned.1.call-done = f32[64,512]{1,0:T(8,128)} async-done(((f32[256,512]{1,0:T(8,128)}), f32[64,512]{1,0:T(8,128)}) %reduce-scatter.16.cloned.1.call-update) | async-done | bytes 131088 | tf_op jit(solution)/shard_map/reduce_scatter | solution.py:117
  292.7 6.0 collective-permute-done.8
  298.8 16.6 %all_to_all.139 = f32[64,4,512]{2,0,1:T(8,128)S(1)} all-to-all(f32[64,4,512]{2,0,1:T(8,128)S(1)} %maximum_select_fusion.3), channel_id=1, replica_groups=mesh['leaf'=8,'panel'=4] {'panel'}, dimensions={1} | all-to-all | bytes 1048576 | tf_op jit(solution)/shard_map/all_to_all | solution.py:55
  315.4 2.4 fusion.76
  319.9 1.9 fusion.28
  321.8 15.1 %reduce-scatter.18.cloned.1.call-done = f32[64,256]{1,0:T(8,128)} async-done(((f32[256,256]{1,0:T(8,128)}), f32[64,256]{1,0:T(8,128)}) %reduce-scatter.18.cloned.1.call-update) | async-done | bytes 65552 | tf_op jit(solution)/shard_map/reduce_scatter | solution.py:124
  338.9 1.6 fusion.2
  340.7 1.5 collective-permute-start.9
  342.3 4.9 collective-permute-done.9
  350.0 3.1 collective-permute-done.10
  358.2 4.1 collective-permute-done.13
  362.3 1.5 collective-permute-start.14
  363.9 6.0 collective-permute-done.14
  370.0 15.8 %all_to_all.140 = f32[64,4,512]{2,0,1:T(8,128)S(1)} all-to-all(f32[64,4,512]{2,0,1:T(8,128)S(1)} %maximum_select_fusion.4), channel_id=1, replica_groups=mesh['leaf'=8,'panel'=4] {'panel'}, dimensions={1} | all-to-all | bytes 1048576 | tf_op jit(solution)/shard_map/all_to_all | solution.py:55
  387.1 19.1 %reduce-scatter.20.cloned.1.call-done = f32[64,256]{1,0:T(8,128)} async-done(((f32[256,256]{1,0:T(8,128)}), f32[64,256]{1,0:T(8,128)}) %reduce-scatter.20.cloned.1.call-update) | async-done | bytes 65552 | tf_op jit(solution)/shard_map/reduce_scatter | solution.py:117
  408.4 1.5 collective-permute-start.16
  409.9 4.1 collective-permute-done.16
  414.0 1.6 collective-permute-start.17
  416.5 5.1 collective-permute-done.17
  421.7 16.5 %all_to_all.141 = f32[64,4,512]{2,0,1:T(8,128)} all-to-all(f32[64,4,512]{2,0,1:T(8,128)S(1)} %maximum_select_fusion.5), channel_id=1, replica_groups=mesh['leaf'=8,'panel'=4] {'panel'}, dimensions={1} | all-to-all | bytes 1048576 | tf_op jit(solution)/shard_map/all_to_all | solution.py:55
  438.2 44.8 %all-gather.9.cloned.1.call-done = f32[256,2048]{1,0:T(8,128)} async-done(((f32[256,512]{1,0:T(8,128)}), f32[256,2048]{1,0:T(8,128)}) %all-gather.9.cloned.1.call-update) | async-done | bytes 2097168 | tf_op jit(solution)/shard_map/all_gather | solution.py:160
  483.0 1.7 fusion.16
  484.9 1.9 collective-permute-done.18
  488.4 12.5 %collective-permute-done.19 = f32[256,512]{1,0:T(8,128)S(1)} collective-permute-done((f32[256,512]{1,0:T(8,128)S(1)}, f32[256,512]{1,0:T(8,128)S(1)}, u32[]{:S(2)}, u32[]{:S(2)}) %collective-permute-start.19) | collective-permute-done | bytes 524320 | tf_op jit(solution)/shard_map/ppermute | solution.py:20
  502.5 11.6 %collective-permute-done.20 = f32[256,512]{1,0:T(8,128)S(1)} collective-permute-done((f32[256,512]{1,0:T(8,128)S(1)}, f32[256,512]{1,0:T(8,128)S(1)}, u32[]{:S(2)}, u32[]{:S(2)}) %collective-permute-start.20) | collective-permute-done | bytes 524320 | tf_op jit(solution)/shard_map/ppermute | solution.py:20
  515.1 44.6 %all-gather.11.cloned.1.call-done = f32[256,2048]{1,0:T(8,128)} async-done(((f32[256,512]{1,0:T(8,128)}), f32[256,2048]{1,0:T(8,128)}) %all-gather.11.cloned.1.call-update) | async-done | bytes 2097168 | tf_op jit(solution)/shard_map/all_gather | solution.py:167
  559.7 1.8 fusion.113
  564.0 1.9 collective-permute-done.21
  567.6 12.5 %collective-permute-done.22 = f32[256,512]{1,0:T(8,128)S(1)} collective-permute-done((f32[256,512]{1,0:T(8,128)S(1)}, f32[256,512]{1,0:T(8,128)S(1)}, u32[]{:S(2)}, u32[]{:S(2)}) %collective-permute-start.22) | collective-permute-done | bytes 524320 | tf_op jit(solution)/shard_map/ppermute | solution.py:20
  581.3 44.4 %all-gather.13.cloned.1.call-done = f32[256,2048]{1,0:T(8,128)} async-done(((f32[256,512]{1,0:T(8,128)}), f32[256,2048]{1,0:T(8,128)}) %all-gather.13.cloned.1.call-update) | async-done | bytes 2097168 | tf_op jit(solution)/shard_map/all_gather | solution.py:160
  625.6 2.5 fusion.11
  628.2 1.9 collective-permute-done.23
  631.7 12.5 %collective-permute-done.24 = f32[256,512]{1,0:T(8,128)S(1)} collective-permute-done((f32[256,512]{1,0:T(8,128)S(1)}, f32[256,512]{1,0:T(8,128)S(1)}, u32[]{:S(2)}, u32[]{:S(2)}) %collective-permute-start.24) | collective-permute-done | bytes 524320 | tf_op jit(solution)/shard_map/ppermute | solution.py:20
  645.1 44.6 %all-gather.15.cloned.1.call-done = f32[256,2048]{1,0:T(8,128)} async-done(((f32[256,512]{1,0:T(8,128)}), f32[256,2048]{1,0:T(8,128)}) %all-gather.15.cloned.1.call-update) | async-done | bytes 2097168 | tf_op jit(solution)/shard_map/all_gather | solution.py:167
  689.7 1.8 fusion.112
  696.7 1.9 collective-permute-done.25
  699.6 44.6 %all-gather.17.cloned.1.call-done = f32[256,2048]{1,0:T(8,128)} async-done(((f32[256,512]{1,0:T(8,128)}), f32[256,2048]{1,0:T(8,128)}) %all-gather.17.cloned.1.call-update) | async-done | bytes 2097168 | tf_op jit(solution)/shard_map/all_gather | solution.py:160
  744.2 3.2 fusion.5
  747.4 1.9 collective-permute-done.26
  750.5 44.3 %all-gather.19.cloned.1.call-done = f32[256,2048]{1,0:T(8,128)} async-done(((f32[256,512]{1,0:T(8,128)}), f32[256,2048]{1,0:T(8,128)}) %all-gather.19.cloned.1.call-update) | async-done | bytes 2097168 | tf_op jit(solution)/shard_map/all_gather | solution.py:167
  794.8 1.8 fusion.111
  801.8 2.8 convolution_subtract_fusion
  804.7 44.6 %all-gather.21.cloned.1.call-done = f32[256,2048]{1,0:T(8,128)} async-done(((f32[256,512]{1,0:T(8,128)}), f32[256,2048]{1,0:T(8,128)}) %all-gather.21.cloned.1.call-update) | async-done | bytes 2097168 | tf_op jit(solution)/shard_map/all_gather | solution.py:160
  849.3 7.3 fusion
  856.6 2.0 broadcast_multiply_fusion.2
  861.9 39.3 %all-gather.23.cloned.1.call-done = f32[256,2048]{1,0:T(8,128)} async-done(((f32[256,512]{1,0:T(8,128)}), f32[256,2048]{1,0:T(8,128)}) %all-gather.23.cloned.1.call-update) | async-done | bytes 2097168 | tf_op jit(solution)/shard_map/all_gather | solution.py:167
  901.2 1.9 dynamic-slice_multiply_fusion.2
  (223 shorter events, 71.6 us)
Async XLA Ops:
  7.2 146.5 %copy-start = (f32[1024,512]{1,0:T(8,128)S(1)}, f32[1024,512]{1,0:T(8,128)}, u32[]{:S(2)}) copy-start(f32[1024,512]{1,0:T(8,128)} %param.20) | copy-start | bytes 6291460
  7.2 74.1 %reduce-scatter.8.cloned.1.call-start = ((), (), s32[]{:S(2)}) async-start(), calls=%async_computation.15 | async-start | bytes 2621440 | tf_op jit(solution)/shard_map/reduce_scatter | solution.py:117
  38.4 90.7 %reduce-scatter.10.cloned.1.call-start = ((), (), s32[]{:S(2)}) async-start(), calls=%async_computation.16 | async-start | bytes 1310720 | tf_op jit(solution)/shard_map/reduce_scatter | solution.py:124
  81.3 18.7 %copy-start.6 = (f32[1024,512]{1,0:T(8,128)S(1)}, f32[1024,512]{1,0:T(8,128)}, u32[]{:S(2)}) copy-start(f32[1024,512]{1,0:T(8,128)} %param.23) | copy-start | bytes 6291460
  100.0 3.0 copy-start.27
  103.0 80.1 %reduce-scatter.12.cloned.1.call-start = ((), (), s32[]{:S(2)}) async-start(), calls=%async_computation.17 | async-start | bytes 1310720 | tf_op jit(solution)/shard_map/reduce_scatter | solution.py:117
  103.2 103.7 %copy-start.24 = (s32[8]{0:T(128)}, s32[8]{0:T(128)S(1)}, u32[]{:S(2)}) copy-start(s32[8]{0:T(128)S(1)} %dynamic-slice_reduce_fusion) | copy-start | bytes 100
  131.5 1.9 collective-permute-start
  132.2 50.9 %copy-start.19 = (f32[1024]{0:T(1024)}, f32[1024]{0:T(1024)S(1)}, u32[]{:S(2)}) copy-start(f32[1024]{0:T(1024)S(1)} %dynamic_slice.72) | copy-start | bytes 12292
  134.5 1.6 collective-permute-start.1
  156.6 70.4 %reduce-scatter.14.cloned.1.call-start = ((), (), s32[]{:S(2)}) async-start(), calls=%async_computation.18 | async-start | bytes 655360 | tf_op jit(solution)/shard_map/reduce_scatter | solution.py:124
  183.1 21.0 %copy-start.13 = (f32[512,512]{1,0:T(8,128)S(1)}, f32[512,512]{1,0:T(8,128)}, u32[]{:S(2)}) copy-start(f32[512,512]{1,0:T(8,128)} %param.24) | copy-start | bytes 3145732
  184.2 1.6 collective-permute-start.2
  206.0 82.0 %reduce-scatter.16.cloned.1.call-start = ((), (), s32[]{:S(2)}) async-start(), calls=%async_computation.19 | async-start | bytes 655360 | tf_op jit(solution)/shard_map/reduce_scatter | solution.py:117
  229.4 6.5 collective-permute-start.3
  235.9 1.4 collective-permute-start.4
  236.7 1.9 copy-start.17
  236.8 1.8 copy-start.21
  236.8 28.2 %copy-start.12 = (f32[512,512]{1,0:T(8,128)S(1)}, f32[512,512]{1,0:T(8,128)}, u32[]{:S(2)}) copy-start(f32[512,512]{1,0:T(8,128)} %param.21) | copy-start | bytes 3145732
  238.3 1.4 collective-permute-start.5
  239.7 8.5 collective-permute-start.6
  248.3 39.7 %copy-start.22 = (f32[512]{0:T(512)S(1)}, f32[512]{0:T(512)}, u32[]{:S(2)}) copy-start(f32[512]{0:T(512)} %copy-done.21) | copy-start | bytes 6148
  266.9 70.0 %reduce-scatter.18.cloned.1.call-start = ((), (), s32[]{:S(2)}) async-start(), calls=%async_computation.20 | async-start | bytes 327680 | tf_op jit(solution)/shard_map/reduce_scatter | solution.py:124
  288.9 1.4 collective-permute-start.7
  290.3 8.4 collective-permute-start.8
  317.8 88.5 %reduce-scatter.20.cloned.1.call-start = ((), (), s32[]{:S(2)}) async-start(), calls=%async_computation.21 | async-start | bytes 327680 | tf_op jit(solution)/shard_map/reduce_scatter | solution.py:117
  340.7 6.4 collective-permute-start.9
  347.9 5.2 collective-permute-start.10
  353.1 1.3 collective-permute-start.11
  355.3 30.4 %copy-start.15 = (f32[256,512]{1,0:T(8,128)S(1)}, f32[256,512]{1,0:T(8,128)}, u32[]{:S(2)}) copy-start(f32[256,512]{1,0:T(8,128)} %param.22) | copy-start | bytes 1572868
  355.3 1.3 collective-permute-start.12
  356.7 5.6 collective-permute-start.13
  362.3 7.6 collective-permute-start.14
  387.1 95.9 %all-gather.9.cloned.1.call-start = ((), (), s32[]{:S(2)}) async-start(), calls=%async_computation.22 | async-start | bytes 2621440 | tf_op jit(solution)/shard_map/all_gather | solution.py:160
  407.1 1.3 collective-permute-start.15
  408.4 5.6 collective-permute-start.16
  414.0 7.6 collective-permute-start.17
  438.2 121.5 %all-gather.11.cloned.1.call-start = ((), (), s32[]{:S(2)}) async-start(), calls=%async_computation.23 | async-start | bytes 2621440 | tf_op jit(solution)/shard_map/all_gather | solution.py:167
  484.8 2.0 collective-permute-start.18
  486.9 14.0 %collective-permute-start.19 = (f32[256,512]{1,0:T(8,128)S(1)}, f32[256,512]{1,0:T(8,128)S(1)}, u32[]{:S(2)}, u32[]{:S(2)}) collective-permute-start(f32[256,512]{1,0:T(8,128)S(1)} %add.290), channel_id=1, source_target_pairs={{0,8},{8,0},{4,12},{12,4},{16,24},{24,16},{20,28},{28,20},{1,9},{9... | collective-permute-start | bytes 1572872 | tf_op jit(solution)/shard_map/ppermute | solution.py:20
  501.0 13.2 %collective-permute-start.20 = (f32[256,512]{1,0:T(8,128)S(1)}, f32[256,512]{1,0:T(8,128)S(1)}, u32[]{:S(2)}, u32[]{:S(2)}) collective-permute-start(f32[256,512]{1,0:T(8,128)S(1)} %add.291), channel_id=1, source_target_pairs={{0,16},{16,0},{4,20},{20,4},{8,24},{24,8},{12,28},{28,12},{1,17},{... | collective-permute-start | bytes 1572872 | tf_op jit(solution)/shard_map/ppermute | solution.py:20
  515.0 110.6 %all-gather.13.cloned.1.call-start = ((), (), s32[]{:S(2)}) async-start(), calls=%async_computation.24 | async-start | bytes 2621440 | tf_op jit(solution)/shard_map/all_gather | solution.py:160
  561.9 4.1 copy-start.1
  563.9 61.7 %copy-start.23 = (f32[512]{0:T(512)S(1)}, f32[512]{0:T(512)}, u32[]{:S(2)}) copy-start(f32[512]{0:T(512)} %copy-done.21) | copy-start | bytes 6148
  564.0 2.0 collective-permute-start.21
  566.0 14.0 %collective-permute-start.22 = (f32[256,512]{1,0:T(8,128)S(1)}, f32[256,512]{1,0:T(8,128)S(1)}, u32[]{:S(2)}, u32[]{:S(2)}) collective-permute-start(f32[256,512]{1,0:T(8,128)S(1)} %add.293), channel_id=1, source_target_pairs={{0,8},{8,0},{4,12},{12,4},{16,24},{24,16},{20,28},{28,20},{1,9},{9... | collective-permute-start | bytes 1572872 | tf_op jit(solution)/shard_map/ppermute | solution.py:20
  581.0 108.7 %all-gather.15.cloned.1.call-start = ((), (), s32[]{:S(2)}) async-start(), calls=%async_computation.25 | async-start | bytes 2621440 | tf_op jit(solution)/shard_map/all_gather | solution.py:167
  628.1 61.6 %copy-start.18 = (f32[2048]{0:T(1024)S(1)}, f32[2048]{0:T(1024)}, u32[]{:S(2)}) copy-start(f32[2048]{0:T(1024)} %copy-done.17) | copy-start | bytes 24580
  628.1 2.0 collective-permute-start.23
  630.2 14.0 %collective-permute-start.24 = (f32[256,512]{1,0:T(8,128)S(1)}, f32[256,512]{1,0:T(8,128)S(1)}, u32[]{:S(2)}, u32[]{:S(2)}) collective-permute-start(f32[256,512]{1,0:T(8,128)S(1)} %add.295), channel_id=1, source_target_pairs={{0,8},{8,0},{4,12},{12,4},{16,24},{24,16},{20,28},{28,20},{1,9},{9... | collective-permute-start | bytes 1572872 | tf_op jit(solution)/shard_map/ppermute | solution.py:20
  645.1 99.1 %all-gather.17.cloned.1.call-start = ((), (), s32[]{:S(2)}) async-start(), calls=%async_computation.26 | async-start | bytes 2621440 | tf_op jit(solution)/shard_map/all_gather | solution.py:160
  691.9 3.2 copy-start.4
  692.0 2.3 copy-start.2
  692.0 2.3 copy-start.29
  694.3 4.3 copy-start.11
  695.5 48.6 %copy-start.20 = (f32[1024]{0:T(1024)S(1)}, f32[1024]{0:T(1024)}, u32[]{:S(2)}) copy-start(f32[1024]{0:T(1024)} %copy-done.19) | copy-start | bytes 12292
  696.6 2.0 collective-permute-start.25
  699.5 95.3 %all-gather.19.cloned.1.call-start = ((), (), s32[]{:S(2)}) async-start(), calls=%async_computation.27 | async-start | bytes 2621440 | tf_op jit(solution)/shard_map/all_gather | solution.py:167
  747.3 2.0 collective-permute-start.26
  750.2 99.1 %all-gather.21.cloned.1.call-start = ((), (), s32[]{:S(2)}) async-start(), calls=%async_computation.28 | async-start | bytes 2621440 | tf_op jit(solution)/shard_map/all_gather | solution.py:160
  797.1 1.6 copy-start.5
  804.7 96.6 %all-gather.23.cloned.1.call-start = ((), (), s32[]{:S(2)}) async-start(), calls=%async_computation.29 | async-start | bytes 2621440 | tf_op jit(solution)/shard_map/all_gather | solution.py:167
  856.6 2.6 copy-start.8
  859.3 1.6 copy-start.9
  (11 other events, 11.2 us)
Sparse Core Ops, SparseCore 0:
  38.5 42.7 reduce-scatter.7
  103.1 25.9 reduce-scatter.9
  156.7 26.3 reduce-scatter.11
  206.1 20.8 reduce-scatter.13
  267.0 20.8 reduce-scatter.15
  317.9 18.9 reduce-scatter.17
  387.2 19.0 reduce-scatter.19
  438.3 44.6 all-gather.8
  515.2 44.4 all-gather.10
  581.1 44.4 all-gather.12
  645.2 44.4 all-gather.14
  699.7 44.4 all-gather.16
  750.3 44.4 all-gather.18
  804.8 44.4 all-gather.20
  856.8 44.4 all-gather.22
where the time goes:
time: 919 us; the launch traced here: 910 us
  waiting for transfers between devices  636 us (69%)
  blocking collectives  139 us (15%)
  matrix products  51.3 us (6%)
  other arithmetic  26.6 us (3%)
  starting transfers between devices  22.5 us (2%)
  between operations  17.9 us (2%)
  local copies, waits for them, and re-layouts  17.6 us (2%)
    all_gather x4, waiting for transfers between devices, local(): lax.all_gather(target, 'panel', axis=1, tiled=True) * node_mask[None, :]  178 us
    all_gather x4, waiting for transfers between devices, local(): lax.all_gather(partial_sum, 'panel', axis=1, tiled=True)  173 us
    all_to_all x8, blocking collectives, to_columns(): lax.all_to_all(full_rows, 'panel', split_axis=1, concat_axis=0, tiled=True)  139 us
    ppermute x27, waiting for transfers between devices, swapped(): return lax.ppermute(block, axis, route)  114 us
    reduce_scatter x4, waiting for transfers between devices, local(): lax.psum_scatter(contract_last(spread, inverse), 'panel', scatter_dimensi...  109 us
    reduce_scatter x3, waiting for transfers between devices, local(): lax.psum_scatter(contract_last(columns, block_rows), 'panel', scatter_dim...  60.5 us
    ppermute x27, starting transfers between devices, swapped(): return lax.ppermute(block, axis, route)  21.3 us
    dot_general x7, matrix products, contract_last(): lax.dot_general(left, right, (((1,), (1,)), ((), ())), precision=highest,...  20.4 us
  transfers between devices with their start and end apart: 42, of which 42 were waited for; matrix products, arithmetic and copies ran while one was open for 1% of the time, Pallas kernels for 0%

commit v1 on v0

v1 whole, which is shorter than its diff:
```python
import jax
import jax.numpy as jnp
from jax import lax
from jax.experimental import pallas as pl
from jax.experimental.pallas import tpu as pltpu
from jax.sharding import PartitionSpec as P

B = 128
LEVELS = 4

high = lax.Precision.HIGH


def swapped(block, bit):
    count = lax.axis_size("leaf")
    route = [(low, low ^ (1 << bit)) for low in range(count)]
    return lax.ppermute(block, "leaf", route)


def pair(is_lower, mine, other, axis):
    return jnp.where(
        is_lower, jnp.concatenate([mine, other], axis), jnp.concatenate([other, mine], axis)
    )


def pick_half(array, which, axis):
    half = array.shape[axis] // 2
    return lax.dynamic_slice_in_dim(array, which * half, half, axis)


def contract_last(left, right):
    return lax.dot_general(
        left, right, (((1,), (1,)), ((), ())), precision=high, preferred_element_type=jnp.float32
    )


def product(left, right):
    return jnp.dot(left, right, precision=high, preferred_element_type=jnp.float32)


class Panel:
    def __init__(self):
        self.count = lax.axis_size("panel")
        self.calls = 0

    def exchange(self, block, out_shape, source, target, summed):
        count = self.count
        self.calls += 1

        def kernel(x_ref, o_ref, *rest):
            if summed:
                held, send_sems, recv_sems = rest
            else:
                held, (send_sems, recv_sems, local_sem) = o_ref, rest
            me = lax.axis_index("panel")
            barrier = pltpu.get_barrier_semaphore()
            for step in range(1, count):
                pl.semaphore_signal(
                    barrier,
                    inc=1,
                    device_id={"panel": lax.rem(me + step, count)},
                    device_id_type=pl.DeviceIdType.MESH,
                )
            if not summed:
                own = pltpu.make_async_copy(source(x_ref, me), target(held, me), local_sem)
                own.start()
            pl.semaphore_wait(barrier, count - 1)
            copies = []
            for step in sorted(range(1, count), key=lambda s: -min(s, count - s)):
                peer = lax.rem(me + step, count)
                copy = pltpu.make_async_remote_copy(
                    src_ref=source(x_ref, peer),
                    dst_ref=held.at[step - 1] if summed else target(held, me),
                    send_sem=send_sems.at[step - 1],
                    recv_sem=recv_sems.at[step - 1],
                    device_id={"panel": peer},
                    device_id_type=pl.DeviceIdType.MESH,
                )
                copy.start()
                copies.append(copy)
            if not summed:
                own.wait()
            for copy in copies:
                copy.wait()
            if summed:
                total = source(x_ref, me)[...]
                for step in range(1, count):
                    total = total + held[step - 1]
                o_ref[...] = total

        sems = [pltpu.SemaphoreType.DMA((count - 1,)), pltpu.SemaphoreType.DMA((count - 1,))]
        if summed:
            scratch = [pltpu.VMEM((count - 1,) + out_shape, jnp.float32)] + sems
        else:
            scratch = sems + [pltpu.SemaphoreType.DMA]
        return pl.pallas_call(
            kernel,
            out_shape=jax.ShapeDtypeStruct(out_shape, jnp.float32),
            in_specs=[pl.BlockSpec(memory_space=pltpu.VMEM)],
            out_specs=pl.BlockSpec(memory_space=pltpu.VMEM),
            scratch_shapes=scratch,
            compiler_params=pltpu.CompilerParams(
                collective_id=self.calls, has_side_effects=True
            ),
            name=f"panel_{self.calls}",
        )(block)

    @staticmethod
    def columns_of(width):
        return lambda ref, who: ref.at[:, pl.ds(pl.multiple_of(who * width, width), width)]

    @staticmethod
    def block_of(ref, who):
        return ref.at[who]

    @staticmethod
    def whole_of(ref, who):
        return ref

    def to_columns(self, rows_form):
        rows, width = rows_form.shape[0], rows_form.shape[1] // self.count
        got = self.exchange(
            rows_form, (self.count, rows, width), self.columns_of(width), self.block_of, False
        )
        return got.reshape(self.count * rows, width)

    def to_rows(self, columns_form):
        rows, width = columns_form.shape[0] // self.count, columns_form.shape[1]
        return self.exchange(
            columns_form.reshape(self.count, rows, width),
            (rows, self.count * width),
            self.block_of,
            self.columns_of(width),
            False,
        )

    def gather(self, columns_form):
        rows, width = columns_form.shape
        return self.exchange(
            columns_form, (rows, self.count * width), self.whole_of, self.columns_of(width), False
        )

    def sum_to_columns(self, partial):
        rows, width = partial.shape[0], partial.shape[1] // self.count
        return self.exchange(
            partial, (rows, width), self.columns_of(width), self.block_of, True
        )

    def sum_to_rows(self, partial):
        rows, width = partial.shape[0] // self.count, partial.shape[1]
        return self.exchange(
            partial.reshape(self.count, rows, width), (rows, width), self.block_of, self.block_of, True
        )


def selector(chosen, tile_total):
    return (chosen[:, None] == jnp.arange(tile_total, dtype=jnp.int32)[None, :]).astype(jnp.float32)


def local(
    live_tiles, row_tiles, rhs0, rhs1, rhs2, rhs3, dinv0, dinv1, dinv2, dinv3, off0, off1, off2
):
    right_sides = [rhs0, rhs1, rhs2, rhs3]
    inverses = [dinv0, dinv1, dinv2, dinv3]
    off_rows = [off0, off1, off2]
    leaf_index = lax.axis_index("leaf")
    panel_index = lax.axis_index("panel")
    leaf_count = lax.axis_size("leaf")
    panel = Panel()
    panel_count = panel.count
    order_rows = dinv0.shape[0]
    width = dinv0.shape[1]
    tile_count = order_rows // B
    bits = [leaf_index // 2**bit % 2 for bit in range(LEVELS)]
    lower = [bit == 0 for bit in bits]
    first_nodes = []
    start_node = 0
    for height in range(LEVELS):
        first_nodes.append(start_node)
        start_node = start_node + leaf_count // 2**height

    def stacked_rows(block, height):
        shape = block.shape
        for place, bit in enumerate(reversed(range(height))):
            mine = jnp.expand_dims(block, place)
            block = pair(lower[bit], mine, jnp.expand_dims(swapped(block, bit), place), place)
        return block.reshape((shape[0] * 2**height, shape[1]))

    def chosen_of(height, flip):
        node = leaf_index // 2**height
        if flip:
            node = node + 1 - 2 * (node % 2)
        return lax.dynamic_index_in_dim(row_tiles, first_nodes[height] + node, keepdims=False)

    residuals = []
    for height in range(LEVELS):
        block = right_sides[height]
        for bit in range(height):
            got = swapped(pick_half(block, 1 - bits[bit], 0), bit)
            block = pair(lower[bit], pick_half(block, bits[bit], 0), got, 1)
        residuals.append(block)
    for height in range(1, LEVELS):
        inverses[height] = stacked_rows(inverses[height], height)
        if height < LEVELS - 1:
            off_rows[height] = stacked_rows(off_rows[height], height)

    masks = []
    own_masks = []
    for height in range(LEVELS):
        live_count = lax.dynamic_index_in_dim(
            live_tiles, first_nodes[height] + leaf_index // 2**height, keepdims=False
        )
        place = jnp.arange(order_rows, dtype=jnp.int32)
        mask = (place < live_count * B).astype(jnp.float32)[None, :]
        masks.append(mask)
        own_masks.append(lax.dynamic_slice_in_dim(mask, panel_index * width, width, 1))

    sums = None
    kept = []
    for height in range(LEVELS):
        residual = residuals[height]
        if sums is not None:
            residual = residual - sums[:, :order_rows]
            sums = sums[:, order_rows:]
        spread = panel.to_columns(residual * masks[height])
        columns = panel.sum_to_columns(contract_last(spread, inverses[height])) * own_masks[height]
        kept.append(columns)
        if height == LEVELS - 1:
            break
        update = panel.sum_to_rows(contract_last(columns, off_rows[height]))
        span = (LEVELS - 1 - height) * tile_count
        chosen = chosen_of(height, False)
        if sums is None:
            got = swapped(pick_half(update, 1 - bits[height], 0), height)
            update = jnp.concatenate([pick_half(update, bits[height], 0), got], 1)
            chosen = jnp.concatenate([chosen, chosen_of(height, True)])
        pieces = update.reshape(update.shape[0], chosen.shape[0], B)
        sent = jnp.einsum("rtb,tc->rcb", pieces, selector(chosen, span), precision=high)
        sent = sent.reshape(update.shape[0], span * B)
        if sums is None:
            sums = sent
        else:
            sums = sums + sent
            got = swapped(pick_half(sums, 1 - bits[height], 0), height)
            sums = pick_half(sums, bits[height], 0) + got

    outputs = [None] * LEVELS
    known = None
    for height in reversed(range(LEVELS)):
        target = kept[height]
        if known is not None:

            def joined(mine, other):
                rows = mine.shape[0] // panel_count
                shape = (panel_count, rows, mine.shape[1])
                both = pair(lower[height], mine.reshape(shape), other.reshape(shape), 1)
                return both.reshape(2 * mine.shape[0], mine.shape[1])

            span = (LEVELS - 1 - height) * tile_count
            tiles = known.reshape(known.shape[0], span, B)

            def selected(flip):
                picked = selector(chosen_of(height, flip), span)
                found = jnp.einsum("rcb,tc->rtb", tiles, picked, precision=high)
                return found.reshape(known.shape[0], picked.shape[0] * B)

            gathered = joined(selected(False), swapped(selected(True), height))
            target = target - product(gathered, off_rows[height])
            if height > 0:
                known = joined(known, swapped(known, height))
        whole_target = panel.gather(target * own_masks[height])
        solved = product(whole_target, inverses[height]) * own_masks[height]
        if height == 0:
            outputs[0] = panel.to_rows(solved)
            break
        whole = panel.gather(solved)
        rows = whole.shape[0] // panel_count
        known = whole if known is None else jnp.concatenate([whole, known], 1)
        block = lax.dynamic_slice_in_dim(whole, panel_index * rows, rows, 0)
        for bit in reversed(range(height)):
            got = swapped(pick_half(block, 1 - bits[bit], 1), bit)
            block = pair(lower[bit], pick_half(block, bits[bit], 1), got, 0)
        outputs[height] = block
    return tuple(outputs)


def solution(mesh):
    vectors = P("panel", "leaf")
    blocks = P("leaf", "panel")
    return jax.shard_map(
        local,
        mesh=mesh,
        in_specs=(P(), P()) + (vectors,) * 4 + (blocks,) * 7,
        out_specs=(vectors,) * 4,
        check_vma=False,
    )
```

time: 919 us -> 571 us (0.62)
  waiting for transfers between devices: 636 us -> 35.1 us
  Pallas kernels: 0 us -> 362 us
  blocking collectives: 139 us -> 0 us
  other arithmetic: 26.6 us -> 59 us
  between operations: 17.9 us -> 4.1 us
  local copies, waits for them, and re-layouts: 17.6 us -> 30.8 us
    pallas_call x0 -> x19, Pallas kernels: none -> 362 us  [exchange(): pl.pallas_call(kernel, out_shape=jax.ShapeDtypeStruct(out_shape, jnp.floa...]
    all_gather x8 -> x0, waiting for transfers between devices: 351 us -> none  [the longest x4 178 us: local(): lax.all_gather(target, 'panel', axis=1, tiled=True) * node_mask[None, :]]
    reduce_scatter x7 -> x0, waiting for transfers between devices: 170 us -> none  [the longest x4 109 us: local(): lax.psum_scatter(contract_last(spread, inverse), 'panel', scatter_dimensi...]
    all_to_all x8 -> x0, blocking collectives: 139 us -> none  [to_columns(): lax.all_to_all(full_rows, 'panel', split_axis=1, concat_axis=0, tiled=True)]
    ppermute x27 -> x29, waiting for transfers between devices: 114 us -> 35.1 us  [swapped(): return lax.ppermute(block, 'leaf', route)]
    select_n x24 -> x27, other arithmetic: 1.97 us -> 44.2 us  [pair(): jnp.where(is_lower, jnp.concatenate([mine, other], axis), jnp.concatenate...]
    dot_general x26 -> x23, matrix products: 51.3 us -> 56.6 us  [the longest x7 26.7 us: product(): jnp.dot(left, right, precision=high, preferred_element_type=jnp.float32)]
    ppermute x27 -> x29, starting transfers between devices: 21.3 us -> 21.2 us  [swapped(): return lax.ppermute(block, 'leaf', route)]
  transfers between devices with their start and end apart: 42 -> 29, of which waited for: 42 -> 9; matrix products, arithmetic and copies ran while one was open for 1% -> 20% of each run, Pallas kernels for 0% -> 47%
where the time goes in v1:
time: 571 us; the launch traced here: 569 us
  Pallas kernels  362 us (63%)
  other arithmetic  59 us (10%)
  matrix products  56.6 us (10%)
  waiting for transfers between devices  35.1 us (6%)
  local copies, waits for them, and re-layouts  30.8 us (5%)
  starting transfers between devices  21.2 us (4%)
    pallas_call x19, Pallas kernels, exchange(): pl.pallas_call(kernel, out_shape=jax.ShapeDtypeStruct(out_shape, jnp.floa...  362 us
    select_n x27, other arithmetic, pair(): jnp.where(is_lower, jnp.concatenate([mine, other], axis), jnp.concatenate...  44.2 us
    ppermute x29, waiting for transfers between devices, swapped(): return lax.ppermute(block, 'leaf', route)  35.1 us
    dot_general x7, matrix products, product(): jnp.dot(left, right, precision=high, preferred_element_type=jnp.float32)  26.7 us
    dot_general x7, matrix products, contract_last(): lax.dot_general(left, right, (((1,), (1,)), ((), ())), precision=high, pr...  24.6 us
    ppermute x29, starting transfers between devices, swapped(): return lax.ppermute(block, 'leaf', route)  21.2 us
    unnamed x85, local copies, waits for them, and re-layouts  15.8 us
  transfers between devices with their start and end apart: 29, of which 9 were waited for; matrix products, arithmetic and copies ran while one was open for 20% of the time, Pallas kernels for 47%

profile of v1, /device:TPU:0, one launch (start us, length us, event | category | flops | bytes accessed | tf_op | source)
XLA Modules:
  0.0 569.3 jit_solution(440600734154103341)
XLA Ops:
  0.6 3.1 collective-permute-start.15
  7.2 1.9 broadcast_multiply_fusion.x_ref
  9.1 15.6 %panel_1.1 = f32[4,64,512]{2,1,0:T(8,128)} custom-call(f32[64,2048]{1,0:T(8,128)} %broadcast_multiply_fusion.x_ref), custom_call_target="tpu_custom_call" | custom-call | tf_op jit(solution)/shard_map/panel_1/pallas_call | solution.py:96
  24.7 5.6 fusion.57.x_ref
  30.2 42.5 %panel_2.1 = f32[256,512]{1,0:T(8,128)} custom-call(f32[256,2048]{1,0:T(8,128)} %fusion.57.x_ref), custom_call_target="tpu_custom_call" | custom-call | tf_op jit(solution)/shard_map/panel_2/pallas_call | solution.py:96
  72.9 3.2 fusion.3
  76.0 32.1 %panel_3.1 = f32[64,1024]{1,0:T(8,128)} custom-call(f32[4,64,1024]{2,1,0:T(8,128)} %bitcast.192), custom_call_target="tpu_custom_call" | custom-call | tf_op jit(solution)/shard_map/panel_3/pallas_call | solution.py:96
  108.1 1.6 constant_dynamic-slice_fusion.23
  118.2 2.4 collective-permute-done.10
  126.8 14.1 %panel_4.1 = f32[4,32,512]{2,1,0:T(8,128)} custom-call(f32[32,2048]{1,0:T(8,128)} %fusion.5.x_ref), custom_call_target="tpu_custom_call" | custom-call | tf_op jit(solution)/shard_map/panel_4/pallas_call | solution.py:96
  143.2 16.3 %collective-permute-done.12 = f32[256,512]{1,0:T(8,128)} collective-permute-done((f32[256,512]{1,0:T(8,128)}, f32[256,512]{1,0:T(8,128)}, u32[]{:S(2)}, u32[]{:S(2)}) %collective-permute-start.12) | collective-permute-done | bytes 524320 | tf_op jit(solution)/shard_map/ppermute | solution.py:17
  160.0 2.8 maximum_select_fusion.10
  162.8 1.7 maximum_select_fusion.9
  164.6 1.6 collective-permute-start.4
  166.2 3.3 maximum_select_fusion.3
  169.4 3.3 maximum_select_fusion.5
  172.7 3.3 maximum_select_fusion.4
  176.0 5.9 %collective-permute-done.16 = f32[2,256,512]{2,1,0:T(8,128)S(1)} collective-permute-done((f32[2,256,512]{2,1,0:T(8,128)S(1)}, f32[2,256,512]{2,1,0:T(8,128)S(1)}, u32[]{:S(2)}, u32[]{:S(2)}) %collective-permute-start.16) | collective-permute-done | bytes 1048608 | tf_op jit(solution)/shard_map/ppermute | solution.py:17
  181.8 1.5 maximum_select_fusion.7
  184.6 3.0 maximum_select_fusion
  187.6 2.0 copy-done.1
  189.6 3.3 fusion.58.x_ref
  192.9 27.1 %panel_5.1 = f32[128,512]{1,0:T(8,128)} custom-call(f32[128,2048]{1,0:T(8,128)} %fusion.58.x_ref), custom_call_target="tpu_custom_call" | custom-call | tf_op jit(solution)/shard_map/panel_5/pallas_call | solution.py:96
  220.9 3.5 fusion.59.x_ref
  224.5 17.8 %panel_6.1 = f32[32,1024]{1,0:T(8,128)} custom-call(f32[4,32,1024]{2,1,0:T(8,128)} %fusion.59.x_ref), custom_call_target="tpu_custom_call" | custom-call | tf_op jit(solution)/shard_map/panel_6/pallas_call | solution.py:96
  246.6 3.4 maximum_select_fusion.6
  250.0 2.7 pad_maximum_fusion
  253.4 8.6 %panel_7.1 = f32[4,16,512]{2,1,0:T(8,128)} custom-call(f32[16,2048]{1,0:T(8,128)} %fusion.7.x_ref), custom_call_target="tpu_custom_call" | custom-call | tf_op jit(solution)/shard_map/panel_7/pallas_call | solution.py:96
  262.0 4.6 maximum_select_fusion.1
  266.6 2.0 copy-done.2
  268.6 2.9 fusion.60.x_ref
  271.6 12.4 %panel_8.1 = f32[64,512]{1,0:T(8,128)} custom-call(f32[64,2048]{1,0:T(8,128)} %fusion.60.x_ref), custom_call_target="tpu_custom_call" | custom-call | tf_op jit(solution)/shard_map/panel_8/pallas_call | solution.py:96
  284.9 3.4 fusion.61.x_ref
  288.3 10.1 %panel_9.1 = f32[16,1024]{1,0:T(8,128)} custom-call(f32[4,16,1024]{2,1,0:T(8,128)} %fusion.61.x_ref), custom_call_target="tpu_custom_call" | custom-call | tf_op jit(solution)/shard_map/panel_9/pallas_call | solution.py:96
  300.2 4.1 copy_select_fusion
  305.0 7.2 %panel_10.1 = f32[4,8,512]{2,1,0:T(8,128)} custom-call(f32[8,2048]{1,0:T(8,128)} %fusion.9.x_ref), custom_call_target="tpu_custom_call" | custom-call | tf_op jit(solution)/shard_map/panel_10/pallas_call | solution.py:96
  312.3 4.6 maximum_select_fusion.2
  316.9 2.1 copy-done.3
  319.0 2.7 fusion.10.x_ref
  321.7 8.5 %panel_11.1 = f32[32,512]{1,0:T(8,128)} custom-call(f32[32,2048]{1,0:T(8,128)} %fusion.10.x_ref), custom_call_target="tpu_custom_call" | custom-call | tf_op jit(solution)/shard_map/panel_11/pallas_call | solution.py:96
  331.7 9.0 %panel_12.1 = f32[32,2048]{1,0:T(8,128)} custom-call(f32[32,512]{1,0:T(8,128)} %multiply_multiply_fusion.x_ref), custom_call_target="tpu_custom_call" | custom-call | tf_op jit(solution)/shard_map/panel_12/pallas_call | solution.py:96
  340.7 4.2 convolution_multiply_fusion.3.x_ref
  344.9 9.1 %panel_13.1 = f32[32,2048]{1,0:T(8,128)} custom-call(f32[32,512]{1,0:T(8,128)} %convolution_multiply_fusion.3.x_ref), custom_call_target="tpu_custom_call" | custom-call | tf_op jit(solution)/shard_map/panel_13/pallas_call | solution.py:96
  355.0 1.6 collective-permute-start.26
  360.1 1.6 collective-permute-start.18
  365.1 3.0 fusion.2.x_ref
  368.1 14.7 %panel_14.1 = f32[64,2048]{1,0:T(8,128)} custom-call(f32[64,512]{1,0:T(8,128)} %fusion.2.x_ref), custom_call_target="tpu_custom_call" | custom-call | tf_op jit(solution)/shard_map/panel_14/pallas_call | solution.py:96
  382.9 4.4 convolution_multiply_fusion.2.x_ref
  387.3 16.4 %panel_15.1 = f32[64,2048]{1,0:T(8,128)} custom-call(f32[64,512]{1,0:T(8,128)} %convolution_multiply_fusion.2.x_ref), custom_call_target="tpu_custom_call" | custom-call | tf_op jit(solution)/shard_map/panel_15/pallas_call | solution.py:96
  406.7 3.5 collective-permute-done.24
  415.8 1.7 reshape_reshape.10
  417.5 3.7 collective-permute-done.20
  422.5 3.0 fusion.1.x_ref
  425.5 23.4 %panel_16.1 = f32[128,2048]{1,0:T(8,128)} custom-call(f32[128,512]{1,0:T(8,128)} %fusion.1.x_ref), custom_call_target="tpu_custom_call" | custom-call | tf_op jit(solution)/shard_map/panel_16/pallas_call | solution.py:96
  448.8 4.5 convolution_multiply_fusion.1.x_ref
  453.3 26.2 %panel_17.1 = f32[128,2048]{1,0:T(8,128)} custom-call(f32[128,512]{1,0:T(8,128)} %convolution_multiply_fusion.1.x_ref), custom_call_target="tpu_custom_call" | custom-call | tf_op jit(solution)/shard_map/panel_17/pallas_call | solution.py:96
  480.8 1.9 maximum_select_fusion.8
  485.7 1.6 maximum_select_fusion.22
  488.0 1.6 convolution_bitcast_fusion
  492.1 1.9 fusion.x_ref
  494.0 44.3 %panel_18.1 = f32[256,2048]{1,0:T(8,128)} custom-call(f32[256,512]{1,0:T(8,128)} %fusion.x_ref), custom_call_target="tpu_custom_call" | custom-call | tf_op jit(solution)/shard_map/panel_18/pallas_call | solution.py:96
  538.4 5.6 convolution_multiply_fusion
  544.0 23.4 %panel_19.1 = f32[64,2048]{1,0:T(8,128)} custom-call(f32[4,64,512]{2,1,0:T(8,128)} %bitcast.204), custom_call_target="tpu_custom_call" | custom-call | tf_op jit(solution)/shard_map/panel_19/pallas_call | solution.py:96
  567.4 1.9 copy.49
  (193 shorter events, 55.5 us)
Async XLA Ops:
  0.6 72.2 %copy-start = (f32[1024,512]{1,0:T(8,128)S(1)}, f32[1024,512]{1,0:T(8,128)}, u32[]{:S(2)}) copy-start(f32[1024,512]{1,0:T(8,128)} %param.23) | copy-start | bytes 6291460
  0.6 140.2 %collective-permute-start.15 = (f32[256,512]{1,0:T(8,128)}, f32[256,512]{1,0:T(8,128)S(1)}, u32[]{:S(2)}, u32[]{:S(2)}) collective-permute-start(f32[256,512]{1,0:T(8,128)} %param.22), channel_id=1, source_target_pairs={{0,16},{4,20},{8,24},{12,28},{16,0},{20,4},{24,8},{28,12},{1,17},{... | collective-permute-start | bytes 1572872 | tf_op jit(solution)/shard_map/ppermute | solution.py:17
  5.1 110.2 %collective-permute-start.9 = (f32[32,256]{1,0:T(8,128)}, f32[32,256]{1,0:T(8,128)}, u32[]{:S(2)}, u32[]{:S(2)}) collective-permute-start(f32[32,256]{1,0:T(8,128)} %get-tuple-element.37), channel_id=1, source_target_pairs={{0,4},{4,0},{8,12},{12,8},{16,20},{20,16},{24,28},{28,24},{1,5},{5... | collective-permute-start | bytes 98312 | tf_op jit(solution)/shard_map/ppermute | solution.py:17
  72.9 36.9 %copy-start.21 = (f32[64,1024]{1,0:T(8,128)S(1)}, f32[64,1024]{1,0:T(8,128)}, u32[]{:S(2)}) copy-start(f32[64,1024]{1,0:T(8,128)} %param.16) | copy-start | bytes 786436
  76.0 35.6 %copy-start.23 = (f32[64,512]{1,0:T(8,128)S(1)}, f32[64,512]{1,0:T(8,128)}, u32[]{:S(2)}) copy-start(f32[64,512]{1,0:T(8,128)} %param.17) | copy-start | bytes 393220
  76.0 37.0 %copy-start.22 = (s32[14,8]{0,1:T(8,128)S(1)}, s32[14,8]{0,1:T(8,128)}, u32[]{:S(2)}) copy-start(s32[14,8]{0,1:T(8,128)} %param.14) | copy-start | bytes 1348
  109.8 12.1 %collective-permute-start.1 = (f32[32,1024]{1,0:T(8,128)}, f32[32,1024]{1,0:T(8,128)}, u32[]{:S(2)}, u32[]{:S(2)}) collective-permute-start(f32[32,1024]{1,0:T(8,128)} %get-tuple-element.21), channel_id=1, source_target_pairs={{0,4},{4,0},{8,12},{12,8},{16,20},{20,16},{24,28},{28,24},{1,5},{5... | collective-permute-start | bytes 393224 | tf_op jit(solution)/shard_map/ppermute | solution.py:17
  110.5 14.7 %collective-permute-start = (f32[32,1024]{1,0:T(8,128)}, f32[32,1024]{1,0:T(8,128)S(1)}, u32[]{:S(2)}, u32[]{:S(2)}) collective-permute-start(f32[32,1024]{1,0:T(8,128)} %get-tuple-element.19), channel_id=1, source_target_pairs={{0,4},{4,0},{8,12},{12,8},{16,20},{20,16},{24,28},{28,24},{1,5},{5... | collective-permute-start | bytes 393224 | tf_op jit(solution)/shard_map/ppermute | solution.py:17
  111.0 72.6 %collective-permute-start.2 = (f32[1024,512]{1,0:T(8,128)}, f32[1024,512]{1,0:T(8,128)}, u32[]{:S(2)}, u32[]{:S(2)}) collective-permute-start(f32[1024,512]{1,0:T(8,128)} %param.20), channel_id=1, source_target_pairs={{0,4},{4,0},{8,12},{12,8},{16,20},{20,16},{24,28},{28,24},{1,5},{5... | collective-permute-start | bytes 6291464 | tf_op jit(solution)/shard_map/ppermute | solution.py:17
  113.8 11.3 %copy-start.32 = (s32[8]{0:T(128)}, s32[8]{0:T(128)S(1)}, u32[]{:S(2)}) copy-start(s32[8]{0:T(128)S(1)} %get-tuple-element.8) | copy-start | bytes 100
  113.8 11.3 %copy-start.34 = (s32[8]{0:T(128)}, s32[8]{0:T(128)S(1)}, u32[]{:S(2)}) copy-start(s32[8]{0:T(128)S(1)} %get-tuple-element.7) | copy-start | bytes 100
  115.3 1.4 collective-permute-start.3
  116.7 3.9 collective-permute-start.10
  120.6 44.0 %collective-permute-start.5 = (f32[512,512]{1,0:T(8,128)}, f32[512,512]{1,0:T(8,128)}, u32[]{:S(2)}, u32[]{:S(2)}) collective-permute-start(f32[512,512]{1,0:T(8,128)} %param.24), channel_id=1, source_target_pairs={{0,4},{4,0},{8,12},{12,8},{16,20},{20,16},{24,28},{28,24},{1,5},{5... | collective-permute-start | bytes 3145736 | tf_op jit(solution)/shard_map/ppermute | solution.py:17
  121.9 47.5 %collective-permute-start.7 = (f32[512,512]{1,0:T(8,128)}, f32[512,512]{1,0:T(8,128)}, u32[]{:S(2)}, u32[]{:S(2)}) collective-permute-start(f32[512,512]{1,0:T(8,128)} %param.21), channel_id=1, source_target_pairs={{0,8},{4,12},{8,0},{12,4},{16,24},{20,28},{24,16},{28,20},{1,9},{5... | collective-permute-start | bytes 3145736 | tf_op jit(solution)/shard_map/ppermute | solution.py:17
  124.4 16.5 %copy-start.6 = (f32[256,512]{1,0:T(8,128)S(1)}, f32[256,512]{1,0:T(8,128)}, u32[]{:S(2)}) copy-start(f32[256,512]{1,0:T(8,128)} %param.22) | copy-start | bytes 1572868
  125.1 0.9 copy-start.12
  125.1 34.3 %collective-permute-start.12 = (f32[256,512]{1,0:T(8,128)}, f32[256,512]{1,0:T(8,128)}, u32[]{:S(2)}, u32[]{:S(2)}) collective-permute-start(f32[256,512]{1,0:T(8,128)} %param.25), channel_id=1, source_target_pairs={{0,8},{4,12},{8,0},{12,4},{16,24},{20,28},{24,16},{28,20},{1,9},{5... | collective-permute-start | bytes 1572872 | tf_op jit(solution)/shard_map/ppermute | solution.py:17
  141.0 40.9 %collective-permute-start.16 = (f32[2,256,512]{2,1,0:T(8,128)S(1)}, f32[2,256,512]{2,1,0:T(8,128)S(1)}, u32[]{:S(2)}, u32[]{:S(2)}) collective-permute-start(f32[2,256,512]{2,1,0:T(8,128)S(1)} %maximum_select_fusion.12), channel_id=1, source_target_pairs={{0,8},{4,12},{8,0},{12,4},{16,24},{20,28},{24,16},{28,20},{1,9},{5... | collective-permute-start | bytes 3145736 | tf_op jit(solution)/shard_map/ppermute | solution.py:17
  142.0 17.5 %copy-start.25 = (f32[8,1024]{1,0:T(8,128)S(1)}, f32[8,1024]{1,0:T(8,128)}, u32[]{:S(2)}) copy-start(f32[8,1024]{1,0:T(8,128)} %get-tuple-element.33) | copy-start | bytes 98308
  159.5 144.9 %collective-permute-start.11 = (f32[8,1024]{1,0:T(8,128)S(1)}, f32[8,1024]{1,0:T(8,128)S(1)}, u32[]{:S(2)}, u32[]{:S(2)}) collective-permute-start(f32[8,1024]{1,0:T(8,128)S(1)} %copy-done.25), channel_id=1, source_target_pairs={{0,16},{4,20},{8,24},{12,28},{16,0},{20,4},{24,8},{28,12},{1,17},{... | collective-permute-start | bytes 98312 | tf_op jit(solution)/shard_map/ppermute | solution.py:17
  160.0 4.6 copy-start.24
  160.0 6.1 %copy-start.17 = (f32[512,512]{1,0:T(8,128)S(1)}, f32[512,512]{1,0:T(8,128)}, u32[]{:S(2)}) copy-start(f32[512,512]{1,0:T(8,128)} %param.24) | copy-start | bytes 3145732
  164.6 88.1 %collective-permute-start.4 = (f32[16,1024]{1,0:T(8,128)S(1)}, f32[16,1024]{1,0:T(8,128)S(1)}, u32[]{:S(2)}, u32[]{:S(2)}) collective-permute-start(f32[16,1024]{1,0:T(8,128)S(1)} %copy-done.24), channel_id=1, source_target_pairs={{0,8},{4,12},{8,0},{12,4},{16,24},{20,28},{24,16},{28,20},{1,9},{5... | collective-permute-start | bytes 196616 | tf_op jit(solution)/shard_map/ppermute | solution.py:17
  166.2 3.3 copy-start.8
  169.4 75.7 %collective-permute-start.13 = (f32[2,256,512]{2,1,0:T(8,128)}, f32[2,256,512]{2,1,0:T(8,128)}, u32[]{:S(2)}, u32[]{:S(2)}) collective-permute-start(f32[2,256,512]{2,1,0:T(8,128)} %maximum_select_fusion.10), channel_id=1, source_target_pairs={{0,4},{4,0},{8,12},{12,8},{16,20},{20,16},{24,28},{28,24},{1,5},{5... | collective-permute-start | bytes 3145736 | tf_op jit(solution)/shard_map/ppermute | solution.py:17
  181.8 1.7 copy-start.9
  181.8 80.2 %collective-permute-start.8 = (f32[2,512,512]{2,1,0:T(8,128)}, f32[2,512,512]{2,1,0:T(8,128)}, u32[]{:S(2)}, u32[]{:S(2)}) collective-permute-start(f32[2,512,512]{2,1,0:T(8,128)} %maximum_select_fusion.5), channel_id=1, source_target_pairs={{0,4},{4,0},{8,12},{12,8},{16,20},{20,16},{24,28},{28,24},{1,5},{5... | collective-permute-start | bytes 6291464 | tf_op jit(solution)/shard_map/ppermute | solution.py:17
  181.8 2.7 copy-start.15
  183.5 128.7 %collective-permute-start.17 = (f32[2,2,256,512]{3,2,1,0:T(8,128)}, f32[2,2,256,512]{3,2,1,0:T(8,128)}, u32[]{:S(2)}, u32[]{:S(2)}) collective-permute-start(f32[2,2,256,512]{3,2,1,0:T(8,128)} %maximum_select_fusion.7), channel_id=1, source_target_pairs={{0,4},{4,0},{8,12},{12,8},{16,20},{20,16},{24,28},{28,24},{1,5},{5... | collective-permute-start | bytes 6291464 | tf_op jit(solution)/shard_map/ppermute | solution.py:17
  184.6 5.0 copy-start.18
  187.6 2.0 copy-start.1
  219.9 23.3 %copy-start.29 = (s32[8]{0:T(128)S(1)}, s32[8]{0:T(128)}, u32[]{:S(2)}) copy-start(s32[8]{0:T(128)} %get-tuple-element.6) | copy-start | bytes 100
  245.1 7.6 %collective-permute-start.6 = (f32[16,4096]{1,0:T(8,128)S(1)}, f32[16,4096]{1,0:T(8,128)S(1)}, u32[]{:S(2)}, u32[]{:S(2)}) collective-permute-start(f32[16,4096]{1,0:T(8,128)S(1)} %constant_dynamic-slice_fusion.16), channel_id=1, source_target_pairs={{0,8},{4,12},{8,0},{12,4},{16,24},{20,28},{24,16},{28,20},{1,9},{5... | collective-permute-start | bytes 786440 | tf_op jit(solution)/shard_map/ppermute | solution.py:17
  246.6 3.4 copy-start.10
  246.6 3.4 copy-start.11
  262.0 6.6 %copy-start.19 = (f32[4,16,512]{2,1,0:T(8,128)S(1)}, f32[4,16,512]{2,1,0:T(8,128)}, u32[]{:S(2)}) copy-start(f32[4,16,512]{2,1,0:T(8,128)} %panel_7.1) | copy-start | bytes 393220
  266.6 2.0 copy-start.2
  268.6 15.3 %copy-start.26 = (f32[512]{0:T(512)S(1)}, f32[512]{0:T(512)}, u32[]{:S(2)}) copy-start(f32[512]{0:T(512)} %dynamic-slice.14) | copy-start | bytes 6148
  271.6 27.6 %copy-start.28 = (s32[8]{0:T(128)S(1)}, s32[8]{0:T(128)}, u32[]{:S(2)}) copy-start(s32[8]{0:T(128)} %get-tuple-element.5) | copy-start | bytes 100
  299.6 4.7 collective-permute-start.14
  312.3 6.7 %copy-start.20 = (f32[4,8,512]{2,1,0:T(8,128)S(1)}, f32[4,8,512]{2,1,0:T(8,128)}, u32[]{:S(2)}) copy-start(f32[4,8,512]{2,1,0:T(8,128)} %panel_10.1) | copy-start | bytes 196612
  316.9 2.1 copy-start.3
  319.0 11.2 %copy-start.27 = (f32[512]{0:T(512)S(1)}, f32[512]{0:T(512)}, u32[]{:S(2)}) copy-start(f32[512]{0:T(512)} %dynamic-slice.15) | copy-start | bytes 6148
  340.7 19.1 %copy-start.31 = (s32[8]{0:T(128)S(1)}, s32[8]{0:T(128)}, u32[]{:S(2)}) copy-start(s32[8]{0:T(128)} %get-tuple-element.9) | copy-start | bytes 100
  344.9 20.2 %copy-start.16 = (f32[64,512]{1,0:T(8,128)S(1)}, f32[64,512]{1,0:T(8,128)}, u32[]{:S(2)}) copy-start(f32[64,512]{1,0:T(8,128)} %panel_8.1) | copy-start | bytes 393220
  355.0 4.0 collective-permute-start.26
  356.6 53.7 %collective-permute-start.19 = (f32[32,2048]{1,0:T(8,128)}, f32[32,2048]{1,0:T(8,128)S(1)}, u32[]{:S(2)}, u32[]{:S(2)}) collective-permute-start(f32[32,2048]{1,0:T(8,128)} %panel_13.1), channel_id=1, source_target_pairs={{0,16},{4,20},{8,24},{12,28},{16,0},{20,4},{24,8},{28,12},{1,17},{... | collective-permute-start | bytes 786440 | tf_op jit(solution)/shard_map/ppermute | solution.py:17
  359.0 4.0 collective-permute-start.27
  360.1 5.0 collective-permute-start.18
  363.1 1.3 collective-permute-start.28
  387.3 23.1 %copy-start.13 = (f32[32,2048]{1,0:T(8,128)S(1)}, f32[32,2048]{1,0:T(8,128)}, u32[]{:S(2)}) copy-start(f32[32,2048]{1,0:T(8,128)} %panel_13.1) | copy-start | bytes 786436
  405.9 4.3 collective-permute-start.24
  406.7 3.9 copy-start.30
  410.2 75.5 %collective-permute-start.25 = (f32[32,512]{1,0:T(8,128)S(1)}, f32[32,512]{1,0:T(8,128)}, u32[]{:S(2)}, u32[]{:S(2)}) collective-permute-start(f32[32,512]{1,0:T(8,128)S(1)} %get-tuple-element.23), channel_id=1, source_target_pairs={{0,4},{4,0},{8,12},{12,8},{16,20},{20,16},{24,28},{28,24},{1,5},{5... | collective-permute-start | bytes 196616 | tf_op jit(solution)/shard_map/ppermute | solution.py:17
  410.4 1.9 copy-start.4
  411.7 9.5 %collective-permute-start.20 = (f32[64,1024]{1,0:T(8,128)}, f32[64,1024]{1,0:T(8,128)}, u32[]{:S(2)}, u32[]{:S(2)}) collective-permute-start(f32[64,1024]{1,0:T(8,128)} %bitcast.165), channel_id=1, source_target_pairs={{0,8},{4,12},{8,0},{12,4},{16,24},{20,28},{24,16},{28,20},{1,9},{5... | collective-permute-start | bytes 786440 | tf_op jit(solution)/shard_map/ppermute | solution.py:17
  412.3 10.1 %copy-start.14 = (f32[128,512]{1,0:T(8,128)S(1)}, f32[128,512]{1,0:T(8,128)}, u32[]{:S(2)}) copy-start(f32[128,512]{1,0:T(8,128)} %panel_5.1) | copy-start | bytes 786436
  413.4 67.4 %collective-permute-start.21 = (f32[64,4096]{1,0:T(8,128)}, f32[64,4096]{1,0:T(8,128)}, u32[]{:S(2)}, u32[]{:S(2)}) collective-permute-start(f32[64,4096]{1,0:T(8,128)} %pad_maximum_fusion.2), channel_id=1, source_target_pairs={{0,8},{4,12},{8,0},{12,4},{16,24},{20,28},{24,16},{28,20},{1,9},{5... | collective-permute-start | bytes 3145736 | tf_op jit(solution)/shard_map/ppermute | solution.py:17
  480.7 6.6 %collective-permute-start.23 = (f32[32,1024]{1,0:T(8,128)S(1)}, f32[32,1024]{1,0:T(8,128)S(1)}, u32[]{:S(2)}, u32[]{:S(2)}) collective-permute-start(f32[32,1024]{1,0:T(8,128)S(1)} %get-tuple-element.13), channel_id=1, source_target_pairs={{0,4},{4,0},{8,12},{12,8},{16,20},{20,16},{24,28},{28,24},{1,5},{5... | collective-permute-start | bytes 393224 | tf_op jit(solution)/shard_map/ppermute | solution.py:17
  480.8 1.9 copy-start.5
  483.6 4.5 copy-start.33
  485.2 5.6 collective-permute-start.22
  489.6 2.5 copy-start.7
  (1 other events, 0.6 us)

commit v2 on v1

--- a/solution.py
+++ b/solution.py
@@ -43,11 +43,20 @@
         self.count = lax.axis_size("panel")
         self.calls = 0
 
-    def exchange(self, block, out_shape, source, target, summed):
+    def exchange(self, block, out_shape, source, target, summed, riders=()):
         count = self.count
         self.calls += 1
-
-        def kernel(x_ref, o_ref, *rest):
+        rider_count = len(riders)
+        widest = max([2**height for _, height, _, _ in riders], default=1)
+
+        def kernel(x_ref, *rest):
+            rider_ins, rest = rest[:rider_count], rest[rider_count:]
+            o_ref, rest = rest[0], rest[1:]
+            rider_outs, rest = rest[:rider_count], rest[rider_count:]
+            if riders:
+                rider_sends, rider_recvs = rest[-2:]
+                rest = rest[:-2]
+            leaf = lax.axis_index("leaf")
             if summed:
                 held, send_sems, recv_sems = rest
             else:
@@ -61,10 +70,17 @@
                     device_id={"panel": lax.rem(me + step, count)},
                     device_id_type=pl.DeviceIdType.MESH,
                 )
+            for step in range(1, widest):
+                pl.semaphore_signal(
+                    barrier,
+                    inc=1,
+                    device_id={"leaf": leaf - leaf % widest + (leaf + step) % widest},
+                    device_id_type=pl.DeviceIdType.MESH,
+                )
             if not summed:
                 own = pltpu.make_async_copy(source(x_ref, me), target(held, me), local_sem)
                 own.start()
-            pl.semaphore_wait(barrier, count - 1)
+            pl.semaphore_wait(barrier, count - 1 + widest - 1)
             copies = []
             for step in sorted(range(1, count), key=lambda s: -min(s, count - s)):
                 peer = lax.rem(me + step, count)
@@ -78,6 +94,21 @@
                 )
                 copy.start()
                 copies.append(copy)
+            slot = 0
+            for number, (_, height, start, wide) in enumerate(riders):
+                group = 2**height
+                for step in range(1, group):
+                    copy = pltpu.make_async_remote_copy(
+                        src_ref=rider_ins[number].at[:, pl.ds(start, wide)],
+                        dst_ref=rider_outs[number].at[leaf % group],
+                        send_sem=rider_sends.at[slot],
+                        recv_sem=rider_recvs.at[slot],
+                        device_id={"leaf": leaf - leaf % group + (leaf + step) % group},
+                        device_id_type=pl.DeviceIdType.MESH,
+                    )
+                    copy.start()
+                    copies.append(copy)
+                    slot += 1
             if not summed:
                 own.wait()
             for copy in copies:
@@ -93,17 +124,35 @@
             scratch = [pltpu.VMEM((count - 1,) + out_shape, jnp.float32)] + sems
         else:
             scratch = sems + [pltpu.SemaphoreType.DMA]
-        return pl.pallas_call(
+        slots = sum(2**height - 1 for _, height, _, _ in riders)
+        if riders:
+            scratch = scratch + [pltpu.SemaphoreType.DMA((slots,)), pltpu.SemaphoreType.DMA((slots,))]
+        rider_shapes = [
+            jax.ShapeDtypeStruct((2**height, array.shape[0], wide), jnp.float32)
+            for array, height, _, wide in riders
+        ]
+        result = pl.pallas_call(
             kernel,
-            out_shape=jax.ShapeDtypeStruct(out_shape, jnp.float32),
-            in_specs=[pl.BlockSpec(memory_space=pltpu.VMEM)],
-            out_specs=pl.BlockSpec(memory_space=pltpu.VMEM),
+            out_shape=[jax.ShapeDtypeStruct(out_shape, jnp.float32)] + rider_shapes,
+            in_specs=[pl.BlockSpec(memory_space=pltpu.VMEM)]
+            + [pl.BlockSpec(memory_space=pl.ANY)] * rider_count,
+            out_specs=[pl.BlockSpec(memory_space=pltpu.VMEM)]
+            + [pl.BlockSpec(memory_space=pl.ANY)] * rider_count,
             scratch_shapes=scratch,
             compiler_params=pltpu.CompilerParams(
                 collective_id=self.calls, has_side_effects=True
             ),
             name=f"panel_{self.calls}",
-        )(block)
+        )(block, *[array for array, _, _, _ in riders])
+        if not riders:
+            return result[0]
+        leaf = lax.axis_index("leaf")
+        whole = []
+        for got, (array, height, start, wide) in zip(result[1:], riders):
+            mine = array[None, :, start : start + wide]
+            full = lax.dynamic_update_slice(got, mine, (leaf % 2**height, 0, 0))
+            whole.append(full.reshape(2**height * array.shape[0], wide))
+        return result[0], whole
 
     @staticmethod
     def columns_of(width):
@@ -117,12 +166,14 @@
     def whole_of(ref, who):
         return ref
 
-    def to_columns(self, rows_form):
+    def to_columns(self, rows_form, riders=()):
         rows, width = rows_form.shape[0], rows_form.shape[1] // self.count
         got = self.exchange(
-            rows_form, (self.count, rows, width), self.columns_of(width), self.block_of, False
-        )
-        return got.reshape(self.count * rows, width)
+            rows_form, (self.count, rows, width), self.columns_of(width), self.block_of, False, riders
+        )
+        if riders:
+            return got[0].reshape(self.count * rows, width), got[1]
+        return got.reshape(self.count * rows, width), []
 
     def to_rows(self, columns_form):
         rows, width = columns_form.shape[0] // self.count, columns_form.shape[1]
@@ -140,17 +191,24 @@
             columns_form, (rows, self.count * width), self.whole_of, self.columns_of(width), False
         )
 
-    def sum_to_columns(self, partial):
+    def sum_to_columns(self, partial, riders=()):
         rows, width = partial.shape[0], partial.shape[1] // self.count
-        return self.exchange(
-            partial, (rows, width), self.columns_of(width), self.block_of, True
-        )
-
-    def sum_to_rows(self, partial):
+        got = self.exchange(
+            partial, (rows, width), self.columns_of(width), self.block_of, True, riders
+        )
+        return got if riders else (got, [])
+
+    def sum_to_rows(self, partial, riders=()):
         rows, width = partial.shape[0] // self.count, partial.shape[1]
-        return self.exchange(
-            partial.reshape(self.count, rows, width), (rows, width), self.block_of, self.block_of, True
-        )
+        got = self.exchange(
+            partial.reshape(self.count, rows, width),
+            (rows, width),
+            self.block_of,
+            self.block_of,
+            True,
+            riders,
+        )
+        return got if riders else (got, [])
 
 
 def selector(chosen, tile_total):
@@ -161,7 +219,6 @@
     live_tiles, row_tiles, rhs0, rhs1, rhs2, rhs3, dinv0, dinv1, dinv2, dinv3, off0, off1, off2
 ):
     right_sides = [rhs0, rhs1, rhs2, rhs3]
-    inverses = [dinv0, dinv1, dinv2, dinv3]
     off_rows = [off0, off1, off2]
     leaf_index = lax.axis_index("leaf")
     panel_index = lax.axis_index("panel")
@@ -179,13 +236,6 @@
         first_nodes.append(start_node)
         start_node = start_node + leaf_count // 2**height
 
-    def stacked_rows(block, height):
-        shape = block.shape
-        for place, bit in enumerate(reversed(range(height))):
-            mine = jnp.expand_dims(block, place)
-            block = pair(lower[bit], mine, jnp.expand_dims(swapped(block, bit), place), place)
-        return block.reshape((shape[0] * 2**height, shape[1]))
-
     def chosen_of(height, flip):
         node = leaf_index // 2**height
         if flip:
@@ -199,10 +249,9 @@
             got = swapped(pick_half(block, 1 - bits[bit], 0), bit)
             block = pair(lower[bit], pick_half(block, bits[bit], 0), got, 1)
         residuals.append(block)
-    for height in range(1, LEVELS):
-        inverses[height] = stacked_rows(inverses[height], height)
-        if height < LEVELS - 1:
-            off_rows[height] = stacked_rows(off_rows[height], height)
+    parts = 2 if width % (2 * B) == 0 else 1
+    part = width // parts
+    inverse_parts = [[dinv0], [], [], []]
 
     masks = []
     own_masks = []
@@ -222,12 +271,39 @@
         if sums is not None:
             residual = residual - sums[:, :order_rows]
             sums = sums[:, order_rows:]
-        spread = panel.to_columns(residual * masks[height])
-        columns = panel.sum_to_columns(contract_last(spread, inverses[height])) * own_masks[height]
+        riders = [(off1, 1, 0, width)] if height == 0 else []
+        spread, found = panel.to_columns(residual * masks[height], riders)
+        if found:
+            off_rows[1] = found[0]
+        wide = width // len(inverse_parts[height])
+        partial = sum(
+            contract_last(spread[:, number * wide : (number + 1) * wide], block)
+            for number, block in enumerate(inverse_parts[height])
+        )
+        riders = []
+        if height == 0:
+            riders = [(dinv1, 1, 0, width), (dinv2, 2, 0, width)]
+        if height == 1:
+            riders = [(dinv3, 3, 0, part)]
+        columns, found = panel.sum_to_columns(partial, riders)
+        if height == 0:
+            inverse_parts[1], inverse_parts[2] = [found[0]], [found[1]]
+        if height == 1:
+            inverse_parts[3] = found
+        columns = columns * own_masks[height]
         kept.append(columns)
         if height == LEVELS - 1:
             break
-        update = panel.sum_to_rows(contract_last(columns, off_rows[height]))
+        riders = []
+        if height == 0:
+            riders = [(off2, 2, 0, width)]
+        if height == 1 and parts == 2:
+            riders = [(dinv3, 3, part, part)]
+        update, found = panel.sum_to_rows(contract_last(columns, off_rows[height]), riders)
+        if height == 0:
+            off_rows[2] = found[0]
+        if height == 1:
+            inverse_parts[3] = inverse_parts[3] + found
         span = (LEVELS - 1 - height) * tile_count
         chosen = chosen_of(height, False)
         if sums is None:
@@ -269,7 +345,8 @@
             if height > 0:
                 known = joined(known, swapped(known, height))
         whole_target = panel.gather(target * own_masks[height])
-        solved = product(whole_target, inverses[height]) * own_masks[height]
+        solved = [product(whole_target, block) for block in inverse_parts[height]]
+        solved = jnp.concatenate(solved, 1) * own_masks[height]
         if height == 0:
             outputs[0] = panel.to_rows(solved)
             break

time: 571 us -> 525 us (0.919)
  other arithmetic: 59 us -> 21 us
  waiting for transfers between devices: 35.1 us -> 20.5 us
  Pallas kernels: 362 us -> 376 us
    select_n x27 -> x14, other arithmetic: 44.2 us -> 9.3 us  [pair(): jnp.where(is_lower, jnp.concatenate([mine, other], axis), jnp.concatenate...]
    ppermute x29 -> x20, waiting for transfers between devices: 35.1 us -> 20.5 us  [swapped(): return lax.ppermute(block, 'leaf', route)]
    pallas_call x19, Pallas kernels: 362 us -> 376 us  [exchange(): pl.pallas_call(kernel, out_shape=[jax.ShapeDtypeStruct(out_shape, jnp.flo...]
    dynamic_update_slice x0 -> x5, local copies, waits for them, and re-layouts: none -> 7.01 us  [exchange(): full = lax.dynamic_update_slice(got, mine, (leaf % 2 ** height, 0, 0))]
    unnamed x85 -> x57, local copies, waits for them, and re-layouts: 15.8 us -> 9.17 us
    dot_general x7 -> x8, matrix products: 24.6 us -> 30.7 us  [contract_last(): lax.dot_general(left, right, (((1,), (1,)), ((), ())), precision=high, pr...]
    ppermute x29 -> x20, starting transfers between devices: 21.2 us -> 15.8 us  [swapped(): return lax.ppermute(block, 'leaf', route)]
    dot_general x7 -> x8, matrix products: 26.7 us -> 25.6 us  [product(): jnp.dot(left, right, precision=high, preferred_element_type=jnp.float32)]
  transfers between devices with their start and end apart: 29 -> 20, of which waited for: 9 -> 8; matrix products, arithmetic and copies ran while one was open for 20% -> 13% of each run, Pallas kernels for 47% -> 34%
where the time goes in v2:
time: 525 us; the launch traced here: 524 us
  Pallas kernels  376 us (72%)
  matrix products  60.1 us (11%)
  local copies, waits for them, and re-layouts  26.1 us (5%)
  other arithmetic  21 us (4%)
  waiting for transfers between devices  20.5 us (4%)
  starting transfers between devices  15.8 us (3%)
    pallas_call x19, Pallas kernels, exchange(): pl.pallas_call(kernel, out_shape=[jax.ShapeDtypeStruct(out_shape, jnp.flo...  376 us
    dot_general x8, matrix products, contract_last(): lax.dot_general(left, right, (((1,), (1,)), ((), ())), precision=high, pr...  30.7 us
    dot_general x8, matrix products, product(): jnp.dot(left, right, precision=high, preferred_element_type=jnp.float32)  25.6 us
    ppermute x20, waiting for transfers between devices, swapped(): return lax.ppermute(block, 'leaf', route)  20.5 us
    ppermute x20, starting transfers between devices, swapped(): return lax.ppermute(block, 'leaf', route)  15.8 us
  transfers between devices with their start and end apart: 20, of which 8 were waited for; matrix products, arithmetic and copies ran while one was open for 13% of the time, Pallas kernels for 34%

profile of v2, /device:TPU:0, one launch (start us, length us, event | category | flops | bytes accessed | tf_op | source)
XLA Modules:
  0.0 523.7 jit_solution(7994429431443647131)
XLA Ops:
  0.7 1.5 fusion.57
  2.9 1.9 broadcast_multiply_fusion.x_ref
  4.8 16.9 %panel_1.1 = (f32[4,64,512]{2,1,0:T(8,128)}, f32[2,512,512]{2,1,0:T(8,128)}) custom-call(f32[64,2048]{1,0:T(8,128)} %broadcast_multiply_fusion.x_ref, f32[512,512]{1,0:T(8,128)} %rest_0_.5), custom_call_target="tpu_custom_call" | custom-call | tf_op jit(solution)/shard_map/panel_1/pallas_call | solution.py:134
  21.7 5.6 %fusion.58.x_ref = f32[256,2048]{1,0:T(8,128)} fusion(f32[256,512]{1,0:T(8,128)} %bitcast.198, f32[2048,512]{1,0:T(8,128)} %param.19), kind=kOutput, calls=%fused_computation.141 | convolution fusion | flops 1610612736 | bytes 6815744 | tf_op jit(solution)/shard_map/dot_general | solution.py:32
  27.3 50.9 %panel_2.1 = (f32[256,512]{1,0:T(8,128)}, f32[2,1024,512]{2,1,0:T(8,128)}, f32[4,512,512]{2,1,0:T(8,128)}) custom-call(f32[256,2048]{1,0:T(8,128)} %fusion.58.x_ref, f32[1024,512]{1,0:T(8,128)} %rest_0_.6, f32[512,512]{1,0:T(8,128)} %rest_1_.1), custom_call_target="tpu_custom_call" | custom-call | tf_op jit(solution)/shard_map/panel_2/pallas_call | solution.py:134
  78.2 3.1 fusion.3
  81.3 28.8 %panel_3.1 = (f32[64,1024]{1,0:T(8,128)}, f32[4,256,512]{2,1,0:T(8,128)}) custom-call(f32[4,64,1024]{2,1,0:T(8,128)} %bitcast.173, f32[256,512]{1,0:T(8,128)} %rest_0_.7), custom_call_target="tpu_custom_call" | custom-call | tf_op jit(solution)/shard_map/panel_3/pallas_call | solution.py:134
  110.1 1.6 constant_dynamic-slice_fusion.23
  111.8 1.5 collective-permute-start.1
  116.4 3.2 bitcast_dynamic-update-slice_fusion
  129.4 1.7 fusion.5.x_ref
  131.1 10.4 %panel_4.1 = f32[4,32,512]{2,1,0:T(8,128)} custom-call(f32[32,2048]{1,0:T(8,128)} %fusion.5.x_ref), custom_call_target="tpu_custom_call" | custom-call | tf_op jit(solution)/shard_map/panel_4/pallas_call | solution.py:134
  141.5 5.5 %fusion.59.x_ref = f32[128,2048]{1,0:T(8,128)} fusion(f32[128,512]{1,0:T(8,128)} %bitcast.192, f32[2048,512]{1,0:T(8,128)} %bitcast.162), kind=kOutput, calls=%fused_computation.142 | convolution fusion | flops 805306368 | bytes 5505024 | tf_op jit(solution)/shard_map/dot_general | solution.py:32
  147.0 27.7 %panel_5.1 = (f32[128,512]{1,0:T(8,128)}, f32[8,256,256]{2,1,0:T(8,128)}) custom-call(f32[128,2048]{1,0:T(8,128)} %fusion.59.x_ref, f32[256,512]{1,0:T(8,128)} %rest_0_.9), custom_call_target="tpu_custom_call" | custom-call | tf_op jit(solution)/shard_map/panel_5/pallas_call | solution.py:134
  175.8 3.5 fusion.60.x_ref
  179.3 28.0 %panel_6.1 = (f32[32,1024]{1,0:T(8,128)}, f32[8,256,256]{2,1,0:T(8,128)}) custom-call(f32[4,32,1024]{2,1,0:T(8,128)} %fusion.60.x_ref, f32[256,512]{1,0:T(8,128)} %rest_0_.9), custom_call_target="tpu_custom_call" | custom-call | tf_op jit(solution)/shard_map/panel_6/pallas_call | solution.py:134
  209.9 1.3 collective-permute-start.3
  212.2 5.8 %collective-permute-done.4 = f32[16,4096]{1,0:T(8,128)S(1)} collective-permute-done((f32[16,4096]{1,0:T(8,128)S(1)}, f32[16,4096]{1,0:T(8,128)S(1)}, u32[]{:S(2)}, u32[]{:S(2)}) %collective-permute-start.4) | collective-permute-done | bytes 262176 | tf_op jit(solution)/shard_map/ppermute | solution.py:17
  218.1 1.4 collective-permute-done.3
  220.1 7.9 %panel_7.1 = f32[4,16,512]{2,1,0:T(8,128)} custom-call(f32[16,2048]{1,0:T(8,128)} %fusion.7.x_ref), custom_call_target="tpu_custom_call" | custom-call | tf_op jit(solution)/shard_map/panel_7/pallas_call | solution.py:134
  228.0 5.1 fusion.61.x_ref
  233.1 13.5 %panel_8.1 = f32[64,512]{1,0:T(8,128)} custom-call(f32[64,2048]{1,0:T(8,128)} %fusion.61.x_ref), custom_call_target="tpu_custom_call" | custom-call | tf_op jit(solution)/shard_map/panel_8/pallas_call | solution.py:134
  247.6 3.4 fusion.62.x_ref
  251.0 10.1 %panel_9.1 = f32[16,1024]{1,0:T(8,128)} custom-call(f32[4,16,1024]{2,1,0:T(8,128)} %fusion.62.x_ref), custom_call_target="tpu_custom_call" | custom-call | tf_op jit(solution)/shard_map/panel_9/pallas_call | solution.py:134
  262.3 1.3 collective-permute-start.8
  264.4 2.2 collective-permute-done.8
  267.3 7.2 %panel_10.1 = f32[4,8,512]{2,1,0:T(8,128)} custom-call(f32[8,2048]{1,0:T(8,128)} %fusion.9.x_ref), custom_call_target="tpu_custom_call" | custom-call | tf_op jit(solution)/shard_map/panel_10/pallas_call | solution.py:134
  274.6 2.8 fusion.11
  277.4 1.7 convolution_add_fusion.x_ref
  279.1 8.6 %panel_11.1 = f32[32,512]{1,0:T(8,128)} custom-call(f32[32,2048]{1,0:T(8,128)} %convolution_add_fusion.x_ref), custom_call_target="tpu_custom_call" | custom-call | tf_op jit(solution)/shard_map/panel_11/pallas_call | solution.py:134
  287.7 1.5 multiply_multiply_fusion.x_ref
  289.2 9.1 %panel_12.1 = f32[32,2048]{1,0:T(8,128)} custom-call(f32[32,512]{1,0:T(8,128)} %multiply_multiply_fusion.x_ref), custom_call_target="tpu_custom_call" | custom-call | tf_op jit(solution)/shard_map/panel_12/pallas_call | solution.py:134
  298.3 2.5 fusion.63
  302.1 9.1 %panel_13.1 = f32[32,2048]{1,0:T(8,128)} custom-call(f32[32,512]{1,0:T(8,128)} %maximum_multiply_fusion.x_ref), custom_call_target="tpu_custom_call" | custom-call | tf_op jit(solution)/shard_map/panel_13/pallas_call | solution.py:134
  312.3 1.2 collective-permute-start.17
  314.5 1.8 collective-permute-done.17
  316.3 1.4 collective-permute-start.18
  318.8 1.5 collective-permute-done.18
  320.6 1.2 collective-permute-start.10
  323.1 3.0 fusion.2.x_ref
  326.1 14.4 %panel_14.1 = f32[64,2048]{1,0:T(8,128)} custom-call(f32[64,512]{1,0:T(8,128)} %fusion.2.x_ref), custom_call_target="tpu_custom_call" | custom-call | tf_op jit(solution)/shard_map/panel_14/pallas_call | solution.py:134
  340.4 4.4 convolution_multiply_fusion.2.x_ref
  344.9 16.2 %panel_15.1 = f32[64,2048]{1,0:T(8,128)} custom-call(f32[64,512]{1,0:T(8,128)} %convolution_multiply_fusion.2.x_ref), custom_call_target="tpu_custom_call" | custom-call | tf_op jit(solution)/shard_map/panel_15/pallas_call | solution.py:134
  361.1 1.1 fusion.55
  362.2 1.1 collective-permute-start.15
  363.3 1.1 copy.25
  364.5 2.0 collective-permute-done.15
  368.0 1.1 collective-permute-start.11
  369.1 1.1 pad_maximum_fusion
  372.2 5.3 %collective-permute-done.11 = f32[64,1024]{1,0:T(8,128)} collective-permute-done((f32[64,1024]{1,0:T(8,128)}, f32[64,1024]{1,0:T(8,128)}, u32[]{:S(2)}, u32[]{:S(2)}) %collective-permute-start.11) | collective-permute-done | bytes 262176 | tf_op jit(solution)/shard_map/ppermute | solution.py:17
  377.5 1.3 maximum_select_fusion.3
  378.8 3.0 fusion.1.x_ref
  381.8 23.4 %panel_16.1 = f32[128,2048]{1,0:T(8,128)} custom-call(f32[128,512]{1,0:T(8,128)} %fusion.1.x_ref), custom_call_target="tpu_custom_call" | custom-call | tf_op jit(solution)/shard_map/panel_16/pallas_call | solution.py:134
  405.2 4.5 convolution_multiply_fusion.1.x_ref
  409.7 26.2 %panel_17.1 = f32[128,2048]{1,0:T(8,128)} custom-call(f32[128,512]{1,0:T(8,128)} %convolution_multiply_fusion.1.x_ref), custom_call_target="tpu_custom_call" | custom-call | tf_op jit(solution)/shard_map/panel_17/pallas_call | solution.py:134
  435.9 1.1 fusion.54
  437.1 1.8 maximum_select_fusion
  441.9 1.6 maximum_select_fusion.10
  445.1 1.4 maximum_select_fusion.1
  446.5 1.9 fusion.x_ref
  448.4 44.3 %panel_18.1 = f32[256,2048]{1,0:T(8,128)} custom-call(f32[256,512]{1,0:T(8,128)} %fusion.x_ref), custom_call_target="tpu_custom_call" | custom-call | tf_op jit(solution)/shard_map/panel_18/pallas_call | solution.py:134
  492.8 5.6 %convolution_multiply_fusion = f32[256,512]{1,0:T(8,128)} fusion(f32[256,2048]{1,0:T(8,128)} %panel_18.1, f32[2048,512]{1,0:T(8,128)} %param.19, f32[512]{0:T(512)S(1)} %dynamic-slice.12), kind=kOutput, calls=%fused_computation.7 | convolution fusion | flops 1610743808 | bytes 6817792 | tf_op jit(solution)/shard_map/dot_general | solution.py:38
  498.4 23.4 %panel_19.1 = f32[64,2048]{1,0:T(8,128)} custom-call(f32[4,64,512]{2,1,0:T(8,128)} %bitcast.183), custom_call_target="tpu_custom_call" | custom-call | tf_op jit(solution)/shard_map/panel_19/pallas_call | solution.py:134
  521.8 1.9 copy.48
  (140 shorter events, 34.0 us)
Async XLA Ops:
  0.6 77.6 %copy-start = (f32[1024,512]{1,0:T(8,128)S(1)}, f32[1024,512]{1,0:T(8,128)}, u32[]{:S(2)}) copy-start(f32[1024,512]{1,0:T(8,128)} %param.23) | copy-start | bytes 6291460
  78.2 35.1 %copy-start.14 = (f32[64,1024]{1,0:T(8,128)S(1)}, f32[64,1024]{1,0:T(8,128)}, u32[]{:S(2)}) copy-start(f32[64,1024]{1,0:T(8,128)} %param.16) | copy-start | bytes 786436
  81.3 32.7 %copy-start.16 = (f32[64,512]{1,0:T(8,128)S(1)}, f32[64,512]{1,0:T(8,128)}, u32[]{:S(2)}) copy-start(f32[64,512]{1,0:T(8,128)} %param.17) | copy-start | bytes 393220
  81.3 33.8 %copy-start.17 = (f32[64,256]{1,0:T(8,128)S(1)}, f32[64,256]{1,0:T(8,128)}, u32[]{:S(2)}) copy-start(f32[64,256]{1,0:T(8,128)} %param.18) | copy-start | bytes 196612
  111.8 15.9 %collective-permute-start.1 = (f32[32,1024]{1,0:T(8,128)}, f32[32,1024]{1,0:T(8,128)}, u32[]{:S(2)}, u32[]{:S(2)}) collective-permute-start(f32[32,1024]{1,0:T(8,128)} %get-tuple-element.43), channel_id=1, source_target_pairs={{0,4},{4,0},{8,12},{12,8},{16,20},{20,16},{24,28},{28,24},{1,5},{5... | collective-permute-start | bytes 393224 | tf_op jit(solution)/shard_map/ppermute | solution.py:17
  114.0 15.4 %collective-permute-start = (f32[32,1024]{1,0:T(8,128)}, f32[32,1024]{1,0:T(8,128)}, u32[]{:S(2)}, u32[]{:S(2)}) collective-permute-start(f32[32,1024]{1,0:T(8,128)} %get-tuple-element.41), channel_id=1, source_target_pairs={{0,4},{4,0},{8,12},{12,8},{16,20},{20,16},{24,28},{28,24},{1,5},{5... | collective-permute-start | bytes 393224 | tf_op jit(solution)/shard_map/ppermute | solution.py:17
  114.6 12.1 %collective-permute-start.2 = (f32[32,512]{1,0:T(8,128)}, f32[32,512]{1,0:T(8,128)}, u32[]{:S(2)}, u32[]{:S(2)}) collective-permute-start(f32[32,512]{1,0:T(8,128)} %get-tuple-element.49), channel_id=1, source_target_pairs={{0,4},{4,0},{8,12},{12,8},{16,20},{20,16},{24,28},{28,24},{1,5},{5... | collective-permute-start | bytes 196616 | tf_op jit(solution)/shard_map/ppermute | solution.py:17
  115.8 9.3 %collective-permute-start.5 = (f32[32,256]{1,0:T(8,128)}, f32[32,256]{1,0:T(8,128)}, u32[]{:S(2)}, u32[]{:S(2)}) collective-permute-start(f32[32,256]{1,0:T(8,128)} %get-tuple-element.59), channel_id=1, source_target_pairs={{0,4},{4,0},{8,12},{12,8},{16,20},{20,16},{24,28},{28,24},{1,5},{5... | collective-permute-start | bytes 98312 | tf_op jit(solution)/shard_map/ppermute | solution.py:17
  116.4 3.2 copy-start.7
  119.7 1.7 copy-start.6
  120.7 3.3 copy-start.15
  121.4 1.2 copy-start.10
  124.2 0.6 copy-start.18
  124.3 0.6 copy-start.20
  125.9 85.3 %collective-permute-start.6 = (f32[16,512]{1,0:T(8,128)S(1)}, f32[16,512]{1,0:T(8,128)S(1)}, u32[]{:S(2)}, u32[]{:S(2)}) collective-permute-start(f32[16,512]{1,0:T(8,128)S(1)} %get-tuple-element.57), channel_id=1, source_target_pairs={{0,8},{4,12},{8,0},{12,4},{16,24},{20,28},{24,16},{28,20},{1,9},{5... | collective-permute-start | bytes 98312 | tf_op jit(solution)/shard_map/ppermute | solution.py:17
  209.0 9.0 %collective-permute-start.4 = (f32[16,4096]{1,0:T(8,128)S(1)}, f32[16,4096]{1,0:T(8,128)S(1)}, u32[]{:S(2)}, u32[]{:S(2)}) collective-permute-start(f32[16,4096]{1,0:T(8,128)S(1)} %constant_dynamic-slice_fusion.16), channel_id=1, source_target_pairs={{0,8},{4,12},{8,0},{12,4},{16,24},{20,28},{24,16},{28,20},{1,9},{5... | collective-permute-start | bytes 786440 | tf_op jit(solution)/shard_map/ppermute | solution.py:17
  209.9 9.6 %collective-permute-start.3 = (f32[16,1024]{1,0:T(8,128)S(1)}, f32[16,1024]{1,0:T(8,128)S(1)}, u32[]{:S(2)}, u32[]{:S(2)}) collective-permute-start(f32[16,1024]{1,0:T(8,128)S(1)} %get-tuple-element.47), channel_id=1, source_target_pairs={{0,8},{4,12},{8,0},{12,4},{16,24},{20,28},{24,16},{28,20},{1,9},{5... | collective-permute-start | bytes 196616 | tf_op jit(solution)/shard_map/ppermute | solution.py:17
  211.2 53.2 %collective-permute-start.7 = (f32[8,1024]{1,0:T(8,128)S(1)}, f32[8,1024]{1,0:T(8,128)S(1)}, u32[]{:S(2)}, u32[]{:S(2)}) collective-permute-start(f32[8,1024]{1,0:T(8,128)S(1)} %get-tuple-element.55), channel_id=1, source_target_pairs={{0,16},{4,20},{8,24},{12,28},{16,0},{20,4},{24,8},{28,12},{1,17},{... | collective-permute-start | bytes 98312 | tf_op jit(solution)/shard_map/ppermute | solution.py:17
  246.6 16.9 %copy-start.5 = (f32[256,512]{1,0:T(8,128)S(1)}, f32[256,512]{1,0:T(8,128)}, u32[]{:S(2)}) copy-start(f32[256,512]{1,0:T(8,128)} %rest_0_.9) | copy-start | bytes 1572868
  262.3 4.3 collective-permute-start.8
  274.5 2.8 copy-start.2
  274.6 2.8 copy-start.13
  298.3 2.5 copy-start.3
  298.3 2.5 copy-start.9
  301.5 21.6 %copy-start.12 = (f32[64,512]{1,0:T(8,128)S(1)}, f32[64,512]{1,0:T(8,128)}, u32[]{:S(2)}) copy-start(f32[64,512]{1,0:T(8,128)} %panel_8.1) | copy-start | bytes 393220
  311.2 9.4 %copy-start.8 = (f32[32,2048]{1,0:T(8,128)S(1)}, f32[32,2048]{1,0:T(8,128)}, u32[]{:S(2)}) copy-start(f32[32,2048]{1,0:T(8,128)} %panel_13.1) | copy-start | bytes 786436
  312.3 4.0 collective-permute-start.17
  316.3 4.0 collective-permute-start.18
  318.0 5.0 collective-permute-start.9
  320.3 1.6 collective-permute-start.19
  320.6 46.0 %collective-permute-start.10 = (f32[32,2048]{1,0:T(8,128)S(1)}, f32[32,2048]{1,0:T(8,128)S(1)}, u32[]{:S(2)}, u32[]{:S(2)}) collective-permute-start(f32[32,2048]{1,0:T(8,128)S(1)} %copy-done.8), channel_id=1, source_target_pairs={{0,16},{4,20},{8,24},{12,28},{16,0},{20,4},{24,8},{28,12},{1,17},{... | collective-permute-start | bytes 786440 | tf_op jit(solution)/shard_map/ppermute | solution.py:17
  362.2 4.3 collective-permute-start.15
  366.6 75.4 %collective-permute-start.16 = (f32[32,512]{1,0:T(8,128)S(1)}, f32[32,512]{1,0:T(8,128)}, u32[]{:S(2)}, u32[]{:S(2)}) collective-permute-start(f32[32,512]{1,0:T(8,128)S(1)} %get-tuple-element.45), channel_id=1, source_target_pairs={{0,4},{4,0},{8,12},{12,8},{16,20},{20,16},{24,28},{28,24},{1,5},{5... | collective-permute-start | bytes 196616 | tf_op jit(solution)/shard_map/ppermute | solution.py:17
  366.7 2.4 copy-start.1
  368.0 9.5 %collective-permute-start.11 = (f32[64,1024]{1,0:T(8,128)}, f32[64,1024]{1,0:T(8,128)}, u32[]{:S(2)}, u32[]{:S(2)}) collective-permute-start(f32[64,1024]{1,0:T(8,128)} %bitcast.156), channel_id=1, source_target_pairs={{0,8},{4,12},{8,0},{12,4},{16,24},{20,28},{24,16},{28,20},{1,9},{5... | collective-permute-start | bytes 786440 | tf_op jit(solution)/shard_map/ppermute | solution.py:17
  370.1 67.0 %collective-permute-start.12 = (f32[64,4096]{1,0:T(8,128)}, f32[64,4096]{1,0:T(8,128)}, u32[]{:S(2)}, u32[]{:S(2)}) collective-permute-start(f32[64,4096]{1,0:T(8,128)} %pad_maximum_fusion), channel_id=1, source_target_pairs={{0,8},{4,12},{8,0},{12,4},{16,24},{20,28},{24,16},{28,20},{1,9},{5... | collective-permute-start | bytes 3145736 | tf_op jit(solution)/shard_map/ppermute | solution.py:17
  437.0 6.5 %collective-permute-start.14 = (f32[32,1024]{1,0:T(8,128)S(1)}, f32[32,1024]{1,0:T(8,128)S(1)}, u32[]{:S(2)}, u32[]{:S(2)}) collective-permute-start(f32[32,1024]{1,0:T(8,128)S(1)} %get-tuple-element.33), channel_id=1, source_target_pairs={{0,4},{4,0},{8,12},{12,8},{16,20},{20,16},{24,28},{28,24},{1,5},{5... | collective-permute-start | bytes 393224 | tf_op jit(solution)/shard_map/ppermute | solution.py:17
  437.1 1.9 copy-start.4
  439.2 0.6 copy-start.21
  439.8 4.5 copy-start.19
  441.4 3.7 collective-permute-start.13
  445.1 1.4 copy-start.11
